TPU v7x, 512 devices: a whole 4x4x16 slice. The times are simulated.
512 devices in a mesh: bead: 16 (over x, z_hi), space: 32 (over z_lo, y, core).
Axes of the slice: x: 4, y: 4, z: 16 (z_hi: 4, z_lo: 4; z = z_hi * 4 + z_lo), core: 2. Of those that a mesh axis runs over, the one named last changes fastest.
Arguments:
- positions: float32 [32, 3, 512, 128], P('bead', None, 'space'), may hold values from -0.1 to 1.1
- momenta: float32 [32, 3, 512, 128], P('bead', None, 'space'), may hold values from -6 to 6
- molecules: int32 [512, 42, 3], P('space'), may hold values from 0 to 128, as said below
Outputs:
- final_positions: float32 [32, 3, 512, 128], P('bead', None, 'space')
- final_momenta: float32 [32, 3, 512, 128], P('bead', None, 'space')
Inputs may be any that keep to these rules, and one draw needn't show every extreme that they name: In each cell, the slots of all listed atoms differ; used molecules come first and unused ones carry 128 in all three places; each cell has 21 to 42 used molecules.
All inputs are finite; a program needn't handle non-finite values.
Results may differ from a plain program's by a relative error of at most 0.0003.
Values sent between devices are 32-bit elements; how exact they have to be, the bound alone decides.
A program may use at most 64 MiB of HBM per device.

v0:
```python
import jax
import jax.numpy as jnp
from jax import lax
from jax.sharding import PartitionSpec as P

REACH = 1
NEIGH = 3


charge_oxygen = -0.8476
charge_hydrogen = 0.4238
coulomb_scale = 24.0
coulomb_soft = 0.004
well_depth = 0.02
sigma_square = 0.0841
lennard_soft = 0.04
bond_stiffness = 20000.0
bond_square = 0.0081
angle_stiffness = 5000.0
angle_square = 0.0204
cycle_frequency = 60.0
outer_step = 0.02
inner_step = 0.01


def padded(cells, sides, width):
    for axis, dim in sides:
        count = lax.axis_size(axis)
        head = lax.slice_in_dim(cells, 0, width, axis=dim)
        tail = lax.slice_in_dim(cells, cells.shape[dim] - width, cells.shape[dim], axis=dim)
        cells = jnp.concatenate(
            [
                lax.ppermute(tail, axis, [(i, (i + 1) % count) for i in range(count)]),
                cells,
                lax.ppermute(head, axis, [((i + 1) % count, i) for i in range(count)]),
            ],
            axis=dim,
        )
    return cells


def sent_together(arrays, axis, split_dim, concat_dim, along):
    both = jnp.concatenate(arrays, axis=along)
    result, at, outs = (
        lax.all_to_all(both, axis, split_axis=split_dim, concat_axis=concat_dim, tiled=True),
        0,
        [],
    )
    for a in arrays:
        outs.append(lax.slice_in_dim(result, at, at + a.shape[along], axis=along))
        at += a.shape[along]
    return tuple(outs)


def entry_shifts(reach):
    return [0] + list(range(-reach, 0)) + list(range(1, reach + 1))


def cell_tables(molecules, slot_count):
    slot_ids = jnp.arange(slot_count, dtype=jnp.int32)
    one_hot = (jnp.transpose(molecules, (0, 2, 1))[..., None] == slot_ids).astype(jnp.float32)
    members = jnp.sum(one_hot, axis=1)
    oxygen = jnp.sum(one_hot[:, 0], axis=1)
    hydrogen = jnp.sum(one_hot[:, 1] + one_hot[:, 2], axis=1)
    charges = charge_oxygen * oxygen + charge_hydrogen * hydrogen
    masses = 1.0 + 15.0 * oxygen
    same_molecule = jnp.einsum("cmi,cmj->cij", members, members, precision=lax.Precision.HIGHEST)
    return (one_hot, oxygen, charges, masses, 1.0 - same_molecule)


def mode_tables(beads):
    bead_ids = jnp.arange(beads, dtype=jnp.int32)
    products = bead_ids[:, None] * bead_ids[None, :] % beads
    angles = 2.0 * jnp.pi / beads * products.astype(jnp.float32)
    columns = bead_ids[None, :]
    half_beads = beads // 2
    transform = jnp.where(
        columns == 0,
        jnp.sqrt(1.0 / beads),
        jnp.where(
            columns < half_beads,
            jnp.sqrt(2.0 / beads) * jnp.cos(angles),
            jnp.where(
                columns == half_beads,
                jnp.sqrt(1.0 / beads) * jnp.cos(angles),
                jnp.sqrt(2.0 / beads) * jnp.sin(angles),
            ),
        ),
    )
    frequencies = 2.0 * cycle_frequency * jnp.sin(jnp.pi * bead_ids.astype(jnp.float32) / beads)
    cosines = jnp.cos(frequencies * inner_step)
    spring_factor = frequencies * jnp.sin(frequencies * inner_step)
    safe_freq = jnp.where(bead_ids == 0, 1.0, frequencies)
    drift_factor = jnp.where(
        bead_ids == 0, inner_step, jnp.sin(frequencies * inner_step) / safe_freq
    )
    return (transform, cosines, spring_factor, drift_factor)


def pair_force(own_atoms, peer_atoms, own_charge, peer_charge, own_oxygen, peer_oxygen, exclusion):
    gap_x = own_atoms[0][:, :, None] - peer_atoms[0][:, None, :]
    gap_y = own_atoms[1][:, :, None] - peer_atoms[1][:, None, :]
    gap_z = own_atoms[2][:, :, None] - peer_atoms[2][:, None, :]
    squares = gap_x * gap_x + gap_y * gap_y + gap_z * gap_z
    charge_pair = own_charge[:, :, None] * peer_charge[:, None, :]
    oxygen_pair = own_oxygen[:, :, None] * peer_oxygen[:, None, :]
    inverse_coulomb = 1.0 / (squares + coulomb_soft)
    coulomb = coulomb_scale * charge_pair * inverse_coulomb * jnp.sqrt(inverse_coulomb)
    inverse_lennard = 1.0 / (squares + lennard_soft)
    sigma_ratio = sigma_square * inverse_lennard
    ratio_cubed = sigma_ratio * sigma_ratio * sigma_ratio
    lennard = (
        24.0
        * well_depth
        * oxygen_pair
        * (2.0 * ratio_cubed * ratio_cubed - ratio_cubed)
        * inverse_lennard
    )
    strength = coulomb + lennard
    if exclusion is not None:
        strength = strength * exclusion
    totals = jnp.sum(strength, axis=2)
    weighted = jnp.einsum("nij,knj->kni", strength, peer_atoms, precision=lax.Precision.HIGHEST)
    return own_atoms * totals[None] - weighted


def bond_forces(coords, one_hot):
    parts = jnp.einsum("ctms,bkcs->tbkcm", one_hot, coords, precision=lax.Precision.HIGHEST)
    first_bond = parts[0] - parts[1]
    second_bond = parts[0] - parts[2]
    third_bond = parts[1] - parts[2]
    first_pull = bond_stiffness * (
        jnp.sum(first_bond * first_bond, axis=1, keepdims=True) - bond_square
    )
    second_pull = bond_stiffness * (
        jnp.sum(second_bond * second_bond, axis=1, keepdims=True) - bond_square
    )
    third_pull = angle_stiffness * (
        jnp.sum(third_bond * third_bond, axis=1, keepdims=True) - angle_square
    )
    on_parts = jnp.stack(
        [
            -first_pull * first_bond - second_pull * second_bond,
            first_pull * first_bond - third_pull * third_bond,
            second_pull * second_bond + third_pull * third_bond,
        ]
    )
    return jnp.einsum("ctms,tbkcm->bkcs", one_hot, on_parts, precision=lax.Precision.HIGHEST)


def free_polymer(coords, moments, masses, transform, cosines, spring_factor, drift_factor):
    shape = coords.shape
    coord_modes = jnp.dot(
        transform.T, coords.reshape(shape[0], -1), precision=lax.Precision.HIGHEST
    ).reshape(shape)
    moment_modes = jnp.dot(
        transform.T, moments.reshape(shape[0], -1), precision=lax.Precision.HIGHEST
    ).reshape(shape)
    weight = masses[None, None]
    cos_col = cosines[:, None, None, None]
    spring_col = spring_factor[:, None, None, None]
    drift_col = drift_factor[:, None, None, None]
    new_moments = cos_col * moment_modes - spring_col * weight * coord_modes
    new_coords = drift_col * moment_modes / weight + cos_col * coord_modes
    coords_out = jnp.dot(
        transform, new_coords.reshape(shape[0], -1), precision=lax.Precision.HIGHEST
    ).reshape(shape)
    moments_out = jnp.dot(
        transform, new_moments.reshape(shape[0], -1), precision=lax.Precision.HIGHEST
    ).reshape(shape)
    return (coords_out, moments_out)


def inter_forces(coords, charges_wide, oxygen_wide, exclusion):
    cell_dev = coords.shape[2]
    unit_x = jnp.array([1.0, 0.0, 0.0], dtype=jnp.float32)[:, None, None]
    widened = padded(coords, (("space", 2),), REACH)
    own_charge = charges_wide[REACH : REACH + cell_dev]
    own_oxygen = oxygen_wide[REACH : REACH + cell_dev]
    total_force = jnp.zeros_like(coords)
    shifts = entry_shifts(REACH)
    for entry_index in range(NEIGH):
        shift_cells = shifts[entry_index]
        first_peer = REACH + shift_cells
        peer_atoms = (
            widened[:, :, first_peer : first_peer + cell_dev] + float(shift_cells) * unit_x[None]
        )
        peer_charge = charges_wide[first_peer : first_peer + cell_dev]
        peer_oxygen = oxygen_wide[first_peer : first_peer + cell_dev]
        excluded = exclusion if entry_index == 0 else None
        bead_forces = lax.map(
            lambda bead_pair: pair_force(
                bead_pair[0],
                bead_pair[1],
                own_charge,
                peer_charge,
                own_oxygen,
                peer_oxygen,
                excluded,
            ),
            (coords, peer_atoms),
        )
        total_force = total_force + bead_forces
    return total_force


def local(positions, momenta, molecules):
    cell_dev = positions.shape[2]
    slot_count = positions.shape[3]
    beads = positions.shape[0] * lax.axis_size("bead")
    group_cells = cell_dev // lax.axis_size("bead")
    wide_molecules = padded(molecules, (("space", 0),), REACH)
    hot_wide, oxygen_wide, charges_wide, masses_wide, exclusion_wide = cell_tables(
        wide_molecules, slot_count
    )
    one_hot = hot_wide[REACH : REACH + cell_dev]
    masses = masses_wide[REACH : REACH + cell_dev]
    exclusion = exclusion_wide[REACH : REACH + cell_dev]
    first_cell = lax.axis_index("bead") * group_cells
    mode_hot = lax.dynamic_slice_in_dim(one_hot, first_cell, group_cells, 0)
    mode_masses = lax.dynamic_slice_in_dim(masses, first_cell, group_cells, 0)
    transform, cosines, spring_factor, drift_factor = mode_tables(beads)
    coords = positions
    moments = momenta
    outer_force = inter_forces(coords, charges_wide, oxygen_wide, exclusion)
    inner_force = None
    moments = moments + 0.5 * outer_step * outer_force
    mode_coords, mode_moments = sent_together((coords, moments), "bead", 2, 0, 1)
    inner_force = bond_forces(mode_coords, mode_hot)
    for inner_index in range(2):
        mode_moments = mode_moments + 0.5 * inner_step * inner_force
        mode_coords, mode_moments = free_polymer(
            mode_coords, mode_moments, mode_masses, transform, cosines, spring_factor, drift_factor
        )
        inner_force = bond_forces(mode_coords, mode_hot)
        mode_moments = mode_moments + 0.5 * inner_step * inner_force
    coords, moments = sent_together((mode_coords, mode_moments), "bead", 0, 2, 1)
    outer_force = inter_forces(coords, charges_wide, oxygen_wide, exclusion)
    moments = moments + 0.5 * outer_step * outer_force
    return (coords, moments)


def solution(mesh):
    in_specs = (
        P("bead", None, "space", None),
        P("bead", None, "space", None),
        P("space", None, None),
    )
    out_specs = (P("bead", None, "space", None), P("bead", None, "space", None))
    return jax.shard_map(local, mesh=mesh, in_specs=in_specs, out_specs=out_specs, check_vma=False)
```

profile of v0, /device:TPU:2, one launch (start us, length us, event | category | flops | bytes accessed | tf_op | source)
XLA Modules:
  0.0 156.6 jit_solution(16554014605788130452)
XLA Ops:
  3.3 8.4 %collective-permute-start.1 = (s32[1,42,3]{1,0,2:T(1,128)S(1)}, s32[1,42,3]{1,0,2:T(1,128)S(1)}, u32[]{:S(2)}, u32[]{:S(2)}) collective-permute-start(s32[1,42,3]{1,0,2:T(1,128)S(1)} %get-tuple-element.757), channel_id=1, source_target_pairs={{1,0},{2,1},{3,2},{4,3},{5,4},{6,5},{7,6},{8,7},{9,8},{10,9},{11,1... | collective-permute-start | bytes 1520 | tf_op jit(solution)/shard_map/ppermute | solution.py:35
  14.4 7.5 %collective-permute-start.3 = (f32[2,3,1,128]{3,2,1,0:T(1,128)S(1)}, f32[2,3,1,128]{3,2,1,0:T(1,128)S(1)}, u32[]{:S(2)}, u32[]{:S(2)}) collective-permute-start(f32[2,3,1,128]{3,2,1,0:T(1,128)S(1)} %get-tuple-element.753), channel_id=1, source_target_pairs={{1,0},{2,1},{3,2},{4,3},{5,4},{6,5},{7,6},{8,7},{9,8},{10,9},{11,1... | collective-permute-start | bytes 9224 | tf_op jit(solution)/shard_map/ppermute | solution.py:35
  27.0 8.0 %while.68 = (s32[]{:T(128)}, f32[2,3,16,128]{3,2,1,0:T(8,128)S(1)}, f32[2,3,16,128]{3,1,2,0:T(4,128)S(1)}, f32[16,128]{1,0:T(8,128)S(1)}, f32[16,128]{1,0:T(8,12...) while((s32[]{:T(128)}, f32[2,3,16,128]{3,2,1,0:T(8,128)S(1)}, ...), condition=%wide.region_5.6_spmd.clone, body=%wide.region_3.5_spmd.clone.sunk | while | flops 17049604 | bytes 3384461 | solution.py:191
  27.1 2.2 %fusion.290 = (f32[16,128]{1,0:T(8,128)S(1)}, f32[16,128,128]{2,1,0:T(8,128)S(1)}) fusion(f32[16,128,128]{2,1,0:T(8,128)S(1)} %get-tuple-element.1176, f32[16,128]{1,0:T(8,128)S(1)} %get-tuple-element.1175, f32[16,128]{1,0:T(8,128)S(1)} %bitcast.388, f32[16,128]{1,0:T(8,128)S(1)} %bitcast.389, f32[16,128]{1,0:T(8,128)S(1)} %bitcast.387, ...), kind=kLoop, calls=%fused_computation.345.clone.1 | loop fusion | flops 7600128 | bytes 2146304 | tf_op jit(solution)/shard_map/while/body/eval_jaxpr/reduce_sum | solution.py:122
  31.1 2.2 %fusion.290 = (f32[16,128]{1,0:T(8,128)S(1)}, f32[16,128,128]{2,1,0:T(8,128)S(1)}) fusion(f32[16,128,128]{2,1,0:T(8,128)S(1)} %get-tuple-element.1176, f32[16,128]{1,0:T(8,128)S(1)} %get-tuple-element.1175, f32[16,128]{1,0:T(8,128)S(1)} %bitcast.388, f32[16,128]{1,0:T(8,128)S(1)} %bitcast.389, f32[16,128]{1,0:T(8,128)S(1)} %bitcast.387, ...), kind=kLoop, calls=%fused_computation.345.clone.1 | loop fusion | flops 7600128 | bytes 2146304 | tf_op jit(solution)/shard_map/while/body/eval_jaxpr/reduce_sum | solution.py:122
  35.2 11.7 %while.64 = (s32[]{:T(128)}, f32[2,3,16,128]{3,2,1,0:T(8,128)S(1)}, f32[2,3,16,128]{3,1,2,0:T(4,128)S(1)}, f32[16,128]{1,0:T(8,128)S(1)}, f32[16,128]{1,0:T(8,12...) while((s32[]{:T(128)}, f32[2,3,16,128]{3,2,1,0:T(8,128)S(1)}, ...), condition=%wide.region_8.9_spmd, body=%wide.region_6.8_spmd.sunk | while | flops 23865348 | bytes 508069 | solution.py:191
  37.5 3.5 %fusion.272 = f32[1,3,16,128]{3,1,2,0:T(4,128)S(1)} fusion(f32[16,128]{1,0:T(8,128)S(1)} %get-tuple-element.1212, f32[16,128]{1,0:T(8,128)S(1)} %get-tuple-element.1211, f32[16,128]{1,0:T(8,128)S(1)} %bitcast.426, f32[16,128]{1,0:T(8,128)S(1)} %bitcast.404, f32[16,128]{1,0:T(8,128)S(1)} %bitcast.434, f32[16,128]{1,0:T(8,128)S(1)} %bitcast.406, ...), kind=kOutput, calls=%fused_computation.4.clone.1 | convolution fusion | flops 16527360 | bytes 163844 | tf_op jit(solution)/shard_map/while/body/eval_jaxpr/nij,knj->kni/dot_general | solution.py:123
  43.3 3.5 %fusion.272 = f32[1,3,16,128]{3,1,2,0:T(4,128)S(1)} fusion(f32[16,128]{1,0:T(8,128)S(1)} %get-tuple-element.1212, f32[16,128]{1,0:T(8,128)S(1)} %get-tuple-element.1211, f32[16,128]{1,0:T(8,128)S(1)} %bitcast.426, f32[16,128]{1,0:T(8,128)S(1)} %bitcast.404, f32[16,128]{1,0:T(8,128)S(1)} %bitcast.434, f32[16,128]{1,0:T(8,128)S(1)} %bitcast.406, ...), kind=kOutput, calls=%fused_computation.4.clone.1 | convolution fusion | flops 16527360 | bytes 163844 | tf_op jit(solution)/shard_map/while/body/eval_jaxpr/nij,knj->kni/dot_general | solution.py:123
  46.9 11.7 %while.65 = (s32[]{:T(128)}, f32[2,3,16,128]{3,2,1,0:T(8,128)S(1)}, f32[2,3,16,128]{3,1,2,0:T(4,128)S(1)}, f32[16,128]{1,0:T(8,128)S(1)}, f32[16,128]{1,0:T(8,12...) while((s32[]{:T(128)}, f32[2,3,16,128]{3,2,1,0:T(8,128)S(1)}, ...), condition=%wide.region_11.12_spmd, body=%wide.region_9.11_spmd.sunk | while | flops 23865348 | bytes 508069 | solution.py:191
  49.2 3.5 %fusion.277 = f32[1,3,16,128]{3,1,2,0:T(4,128)S(1)} fusion(f32[16,128]{1,0:T(8,128)S(1)} %get-tuple-element.1146, f32[16,128]{1,0:T(8,128)S(1)} %get-tuple-element.1145, f32[16,128]{1,0:T(8,128)S(1)} %bitcast.428, f32[16,128]{1,0:T(8,128)S(1)} %bitcast.410, f32[16,128]{1,0:T(8,128)S(1)} %bitcast.436, f32[16,128]{1,0:T(8,128)S(1)} %bitcast.412, ...), kind=kOutput, calls=%fused_computation.28.clone.1 | convolution fusion | flops 16527360 | bytes 163844 | tf_op jit(solution)/shard_map/while/body/eval_jaxpr/nij,knj->kni/dot_general | solution.py:123
  55.1 3.5 %fusion.277 = f32[1,3,16,128]{3,1,2,0:T(4,128)S(1)} fusion(f32[16,128]{1,0:T(8,128)S(1)} %get-tuple-element.1146, f32[16,128]{1,0:T(8,128)S(1)} %get-tuple-element.1145, f32[16,128]{1,0:T(8,128)S(1)} %bitcast.428, f32[16,128]{1,0:T(8,128)S(1)} %bitcast.410, f32[16,128]{1,0:T(8,128)S(1)} %bitcast.436, f32[16,128]{1,0:T(8,128)S(1)} %bitcast.412, ...), kind=kOutput, calls=%fused_computation.28.clone.1 | convolution fusion | flops 16527360 | bytes 163844 | tf_op jit(solution)/shard_map/while/body/eval_jaxpr/nij,knj->kni/dot_general | solution.py:123
  59.3 17.2 %all-to-all-start = ((f32[2,6,16,128]{3,1,0,2:T(8,128)}), f32[2,6,16,128]{3,1,0,2:T(8,128)S(1)}, u32[]{:S(2)}, u32[]{:S(2)}) async-start(f32[2,6,16,128]{3,1,0,2:T(8,128)} %copy.169), calls=%async_computation | async-start | bytes 262144 | tf_op jit(solution)/shard_map/all_to_all | solution.py:45
  76.7 13.6 %all-to-all-done = f32[2,6,16,128]{3,1,0,2:T(8,128)S(1)} async-done(((f32[2,6,16,128]{3,1,0,2:T(8,128)}), f32[2,6,16,128]{3,1,0,2:T(8,128)S(1)}, u32[]{:S(2)}, u32[]{:S(2)}) %all-to-all-start) | async-done | bytes 98336 | tf_op jit(solution)/shard_map/all_to_all | solution.py:45
  95.6 5.5 %all-to-all-start.1 = ((f32[32,6,1,128]{3,2,1,0:T(1,128)}), f32[32,6,1,128]{3,2,1,0:T(1,128)S(1)}, u32[]{:S(2)}, u32[]{:S(2)}) async-start(f32[32,6,1,128]{3,2,1,0:T(1,128)} %copy.178), calls=%async_computation.1 | async-start | bytes 196608 | tf_op jit(solution)/shard_map/all_to_all | solution.py:45
  101.1 13.5 %all-to-all-done.1 = f32[32,6,1,128]{3,2,1,0:T(1,128)S(1)} async-done(((f32[32,6,1,128]{3,2,1,0:T(1,128)}), f32[32,6,1,128]{3,2,1,0:T(1,128)S(1)}, u32[]{:S(2)}, u32[]{:S(2)}) %all-to-all-start.1) | async-done | bytes 98336 | tf_op jit(solution)/shard_map/all_to_all | solution.py:45
  116.6 7.7 %collective-permute-start.5 = (f32[2,3,1,128]{3,2,1,0:T(1,128)S(1)}, f32[2,3,1,128]{3,2,1,0:T(1,128)S(1)}, u32[]{:S(2)}, u32[]{:S(2)}) collective-permute-start(f32[2,3,1,128]{3,2,1,0:T(1,128)S(1)} %get-tuple-element.747), channel_id=1, source_target_pairs={{1,0},{2,1},{3,2},{4,3},{5,4},{6,5},{7,6},{8,7},{9,8},{10,9},{11,1... | collective-permute-start | bytes 9224 | tf_op jit(solution)/shard_map/ppermute | solution.py:35
  124.4 8.0 %while.69 = (s32[]{:T(128)}, f32[2,3,16,128]{3,2,1,0:T(8,128)S(1)}, f32[2,3,16,128]{3,1,2,0:T(4,128)S(1)}, f32[16,128]{1,0:T(8,128)S(1)}, f32[16,128]{1,0:T(8,12...) while((s32[]{:T(128)}, f32[2,3,16,128]{3,2,1,0:T(8,128)S(1)}, ...), condition=%wide.region_23.24_spmd.clone, body=%wide.region_21.23_spmd.clone.sunk | while | flops 17049604 | bytes 3384461 | solution.py:191
  124.4 2.2 %fusion.294 = (f32[16,128]{1,0:T(8,128)S(1)}, f32[16,128,128]{2,1,0:T(8,128)S(1)}) fusion(f32[16,128,128]{2,1,0:T(8,128)S(1)} %get-tuple-element.1278, f32[16,128]{1,0:T(8,128)S(1)} %get-tuple-element.1277, f32[16,128]{1,0:T(8,128)S(1)} %bitcast.391, f32[16,128]{1,0:T(8,128)S(1)} %bitcast.392, f32[16,128]{1,0:T(8,128)S(1)} %bitcast.390, ...), kind=kLoop, calls=%fused_computation.346.clone.1 | loop fusion | flops 7600128 | bytes 2146304 | tf_op jit(solution)/shard_map/while/body/eval_jaxpr/reduce_sum | solution.py:122
  132.5 11.7 %while.66 = (s32[]{:T(128)}, f32[2,3,16,128]{3,2,1,0:T(8,128)S(1)}, f32[2,3,16,128]{3,1,2,0:T(4,128)S(1)}, f32[16,128]{1,0:T(8,128)S(1)}, f32[16,128]{1,0:T(8,12...) while((s32[]{:T(128)}, f32[2,3,16,128]{3,2,1,0:T(8,128)S(1)}, ...), condition=%wide.region_26.27_spmd, body=%wide.region_24.26_spmd.sunk | while | flops 23865348 | bytes 508069 | solution.py:191
  134.8 3.5 %fusion.282 = f32[1,3,16,128]{3,1,2,0:T(4,128)S(1)} fusion(f32[16,128]{1,0:T(8,128)S(1)} %get-tuple-element.1314, f32[16,128]{1,0:T(8,128)S(1)} %get-tuple-element.1313, f32[16,128]{1,0:T(8,128)S(1)} %bitcast.430, f32[16,128]{1,0:T(8,128)S(1)} %bitcast.416, f32[16,128]{1,0:T(8,128)S(1)} %bitcast.438, f32[16,128]{1,0:T(8,128)S(1)} %bitcast.418, ...), kind=kOutput, calls=%fused_computation.52.clone.1 | convolution fusion | flops 16527360 | bytes 163844 | tf_op jit(solution)/shard_map/while/body/eval_jaxpr/nij,knj->kni/dot_general | solution.py:123
  140.7 3.5 %fusion.282 = f32[1,3,16,128]{3,1,2,0:T(4,128)S(1)} fusion(f32[16,128]{1,0:T(8,128)S(1)} %get-tuple-element.1314, f32[16,128]{1,0:T(8,128)S(1)} %get-tuple-element.1313, f32[16,128]{1,0:T(8,128)S(1)} %bitcast.430, f32[16,128]{1,0:T(8,128)S(1)} %bitcast.416, f32[16,128]{1,0:T(8,128)S(1)} %bitcast.438, f32[16,128]{1,0:T(8,128)S(1)} %bitcast.418, ...), kind=kOutput, calls=%fused_computation.52.clone.1 | convolution fusion | flops 16527360 | bytes 163844 | tf_op jit(solution)/shard_map/while/body/eval_jaxpr/nij,knj->kni/dot_general | solution.py:123
  144.2 11.7 %while.67 = (s32[]{:T(128)}, f32[2,3,16,128]{3,2,1,0:T(8,128)S(1)}, f32[2,3,16,128]{3,1,2,0:T(4,128)S(1)}, f32[16,128]{1,0:T(8,128)S(1)}, f32[16,128]{1,0:T(8,12...) while((s32[]{:T(128)}, f32[2,3,16,128]{3,2,1,0:T(8,128)S(1)}, ...), condition=%wide.region_29.30_spmd, body=%wide.region_27.29_spmd.sunk | while | flops 23865348 | bytes 508069 | solution.py:191
  146.5 3.5 %fusion.287 = f32[1,3,16,128]{3,1,2,0:T(4,128)S(1)} fusion(f32[16,128]{1,0:T(8,128)S(1)} %get-tuple-element.1248, f32[16,128]{1,0:T(8,128)S(1)} %get-tuple-element.1247, f32[16,128]{1,0:T(8,128)S(1)} %bitcast.432, f32[16,128]{1,0:T(8,128)S(1)} %bitcast.422, f32[16,128]{1,0:T(8,128)S(1)} %bitcast.440, f32[16,128]{1,0:T(8,128)S(1)} %bitcast.424, ...), kind=kOutput, calls=%fused_computation.76.clone.1 | convolution fusion | flops 16527360 | bytes 163844 | tf_op jit(solution)/shard_map/while/body/eval_jaxpr/nij,knj->kni/dot_general | solution.py:123
  152.4 3.5 %fusion.287 = f32[1,3,16,128]{3,1,2,0:T(4,128)S(1)} fusion(f32[16,128]{1,0:T(8,128)S(1)} %get-tuple-element.1248, f32[16,128]{1,0:T(8,128)S(1)} %get-tuple-element.1247, f32[16,128]{1,0:T(8,128)S(1)} %bitcast.432, f32[16,128]{1,0:T(8,128)S(1)} %bitcast.422, f32[16,128]{1,0:T(8,128)S(1)} %bitcast.440, f32[16,128]{1,0:T(8,128)S(1)} %bitcast.424, ...), kind=kOutput, calls=%fused_computation.76.clone.1 | convolution fusion | flops 16527360 | bytes 163844 | tf_op jit(solution)/shard_map/while/body/eval_jaxpr/nij,knj->kni/dot_general | solution.py:123
  (170 shorter events, 46.3 us)
Async XLA Ops:
  1.4 21.6 %collective-permute-start = (s32[1,42,3]{1,0,2:T(1,128)S(1)}, s32[1,42,3]{1,0,2:T(1,128)S(1)}, u32[]{:S(2)}, u32[]{:S(2)}) collective-permute-start(s32[1,42,3]{1,0,2:T(1,128)S(1)} %get-tuple-element.756), channel_id=1, source_target_pairs={{0,1},{1,2},{2,3},{3,4},{4,5},{5,6},{6,7},{7,8},{8,9},{9,10},{10,1... | collective-permute-start | bytes 1520 | tf_op jit(solution)/shard_map/ppermute | solution.py:33
  3.3 19.7 %collective-permute-start.1 = (s32[1,42,3]{1,0,2:T(1,128)S(1)}, s32[1,42,3]{1,0,2:T(1,128)S(1)}, u32[]{:S(2)}, u32[]{:S(2)}) collective-permute-start(s32[1,42,3]{1,0,2:T(1,128)S(1)} %get-tuple-element.757), channel_id=1, source_target_pairs={{1,0},{2,1},{3,2},{4,3},{5,4},{6,5},{7,6},{8,7},{9,8},{10,9},{11,1... | collective-permute-start | bytes 1520 | tf_op jit(solution)/shard_map/ppermute | solution.py:35
  12.5 22.6 %collective-permute-start.2 = (f32[2,3,1,128]{3,2,1,0:T(1,128)S(1)}, f32[2,3,1,128]{3,2,1,0:T(1,128)S(1)}, u32[]{:S(2)}, u32[]{:S(2)}) collective-permute-start(f32[2,3,1,128]{3,2,1,0:T(1,128)S(1)} %get-tuple-element.752), channel_id=1, source_target_pairs={{0,1},{1,2},{2,3},{3,4},{4,5},{5,6},{6,7},{7,8},{8,9},{9,10},{10,1... | collective-permute-start | bytes 9224 | tf_op jit(solution)/shard_map/ppermute | solution.py:33
  14.4 20.6 %collective-permute-start.3 = (f32[2,3,1,128]{3,2,1,0:T(1,128)S(1)}, f32[2,3,1,128]{3,2,1,0:T(1,128)S(1)}, u32[]{:S(2)}, u32[]{:S(2)}) collective-permute-start(f32[2,3,1,128]{3,2,1,0:T(1,128)S(1)} %get-tuple-element.753), channel_id=1, source_target_pairs={{1,0},{2,1},{3,2},{4,3},{5,4},{6,5},{7,6},{8,7},{9,8},{10,9},{11,1... | collective-permute-start | bytes 9224 | tf_op jit(solution)/shard_map/ppermute | solution.py:35
  27.0 8.0 %copy-start = (f32[2,3,16,128]{3,2,1,0:T(8,128)S(1)}, f32[2,3,16,128]{3,2,1,0:T(8,128)}, u32[]{:S(2)}) copy-start(f32[2,3,16,128]{3,2,1,0:T(8,128)} %param.17) | copy-start | bytes 147460
  27.0 8.0 %copy-start.3 = (f32[3]{0:T(128)S(1)}, f32[3]{0:T(128)}, u32[]{:S(2)}) copy-start(f32[3]{0:T(128)} %constant.254.clone) | copy-start | bytes 40
  27.0 8.0 %copy-start.4 = (f32[3]{0:T(128)S(1)}, f32[3]{0:T(128)}, u32[]{:S(2)}) copy-start(f32[3]{0:T(128)} %constant.259) | copy-start | bytes 40
  46.9 11.7 %copy-start.2 = (f32[2,3,16,128]{3,2,1,0:T(8,128)S(1)}, f32[2,3,16,128]{3,2,1,0:T(8,128)}, u32[]{:S(2)}) copy-start(f32[2,3,16,128]{3,2,1,0:T(8,128)} %param.18) | copy-start | bytes 147460
  59.3 31.0 %all-to-all-start = ((f32[2,6,16,128]{3,1,0,2:T(8,128)}), f32[2,6,16,128]{3,1,0,2:T(8,128)S(1)}, u32[]{:S(2)}, u32[]{:S(2)}) async-start(f32[2,6,16,128]{3,1,0,2:T(8,128)} %copy.169), calls=%async_computation | async-start | bytes 262144 | tf_op jit(solution)/shard_map/all_to_all | solution.py:45
  95.6 19.0 %all-to-all-start.1 = ((f32[32,6,1,128]{3,2,1,0:T(1,128)}), f32[32,6,1,128]{3,2,1,0:T(1,128)S(1)}, u32[]{:S(2)}, u32[]{:S(2)}) async-start(f32[32,6,1,128]{3,2,1,0:T(1,128)} %copy.178), calls=%async_computation.1 | async-start | bytes 196608 | tf_op jit(solution)/shard_map/all_to_all | solution.py:45
  114.6 17.8 %copy-start.1 = (f32[2,3,16,128]{3,2,1,0:T(8,128)}, f32[2,3,16,128]{3,2,1,0:T(8,128)S(1)}, u32[]{:S(2)}) copy-start(f32[2,3,16,128]{3,2,1,0:T(8,128)S(1)} %slice.368) | copy-start | bytes 147460
  114.7 17.7 %collective-permute-start.4 = (f32[2,3,1,128]{3,2,1,0:T(1,128)S(1)}, f32[2,3,1,128]{3,2,1,0:T(1,128)S(1)}, u32[]{:S(2)}, u32[]{:S(2)}) collective-permute-start(f32[2,3,1,128]{3,2,1,0:T(1,128)S(1)} %get-tuple-element.746), channel_id=1, source_target_pairs={{0,1},{1,2},{2,3},{3,4},{4,5},{5,6},{6,7},{7,8},{8,9},{9,10},{10,1... | collective-permute-start | bytes 9224 | tf_op jit(solution)/shard_map/ppermute | solution.py:33
  116.6 15.8 %collective-permute-start.5 = (f32[2,3,1,128]{3,2,1,0:T(1,128)S(1)}, f32[2,3,1,128]{3,2,1,0:T(1,128)S(1)}, u32[]{:S(2)}, u32[]{:S(2)}) collective-permute-start(f32[2,3,1,128]{3,2,1,0:T(1,128)S(1)} %get-tuple-element.747), channel_id=1, source_target_pairs={{1,0},{2,1},{3,2},{4,3},{5,4},{6,5},{7,6},{8,7},{9,8},{10,9},{11,1... | collective-permute-start | bytes 9224 | tf_op jit(solution)/shard_map/ppermute | solution.py:35
where the time goes:
time: 157 us
  starting transfers between devices  52.1 us (33%)
  matrix products  41.1 us (26%)
  other arithmetic  29.3 us (19%)
  waiting for transfers between devices  27.2 us (17%)
  local copies, waits for them, and re-layouts  4.91 us (3%)
    dot_general x12, matrix products, pair_force(): jnp.einsum('nij,knj->kni', strength, peer_atoms, precision=lax.Precision....  35.2 us
    all_to_all x2, waiting for transfers between devices, sent_together(): lax.all_to_all(both, axis, split_axis=split_dim, concat_axis=concat_dim,...  27.1 us
    reduce_sum x12, other arithmetic, pair_force(): totals = jnp.sum(strength, axis=2)  26.1 us
    ppermute x3, starting transfers between devices, padded(): lax.ppermute(head, axis, [((i + 1) % count, i) for i in range(count)])  23.7 us
    all_to_all x2, starting transfers between devices, sent_together(): lax.all_to_all(both, axis, split_axis=split_dim, concat_axis=concat_dim,...  22.7 us
    ppermute x3, starting transfers between devices, padded(): lax.ppermute(tail, axis, [(i, (i + 1) % count) for i in range(count)])  5.74 us
  transfers between devices with their start and end apart: 8, of which 2 were waited for; matrix products, arithmetic and copies ran while one was open for 14% of the time, Pallas kernels for 0%

commit v1 on v0

v1 whole, which is shorter than its diff:
```python
import functools

import jax
import jax.numpy as jnp
import numpy as np
from jax import lax
from jax.experimental import pallas as pl
from jax.experimental.pallas import tpu as pltpu
from jax.sharding import PartitionSpec as P

MESH = pl.DeviceIdType.MESH

SLOTS = 128
MOLS = 42
CELLS = 16
BEADS = 32
GROUP = 16
SPACE = 32
FLIP = 16

charge_oxygen = -0.8476
charge_hydrogen = 0.4238
coulomb_scale = 24.0
coulomb_soft = 0.004
well_depth = 0.02
sigma_square = 0.0841
lennard_soft = 0.04
bond_stiffness = 20000.0
bond_square = 0.0081
angle_stiffness = 5000.0
angle_square = 0.0204
cycle_frequency = 60.0
outer_step = 0.02
inner_step = 0.01
BIG = 2.0**100

f32 = jnp.float32
bf16 = jnp.bfloat16


def propagators():
    ids = np.arange(BEADS)
    angles = 2.0 * np.pi / BEADS * (ids[:, None] * ids[None, :] % BEADS)
    half = BEADS // 2
    col = ids[None, :]
    transform = np.where(
        col == 0,
        np.sqrt(1.0 / BEADS),
        np.where(
            col < half,
            np.sqrt(2.0 / BEADS) * np.cos(angles),
            np.where(
                col == half,
                np.sqrt(1.0 / BEADS) * np.cos(angles),
                np.sqrt(2.0 / BEADS) * np.sin(angles),
            ),
        ),
    )
    freq = 2.0 * cycle_frequency * np.sin(np.pi * ids / BEADS)
    cosk = np.cos(freq * inner_step)
    springk = freq * np.sin(freq * inner_step)
    driftk = np.where(ids == 0, inner_step, np.sin(freq * inner_step) / np.where(ids == 0, 1.0, freq))
    on = [transform @ np.diag(v) @ transform.T for v in (cosk, driftk, -springk)]
    step = [[on[0], on[1]], [on[2], on[0]]]
    tile = np.zeros((2, 3, BEADS), int)
    plane = np.zeros((2, 3, BEADS), int)
    for kind in range(2):
        for k in range(3):
            for j in range(BEADS):
                tile[kind, k, j] = 128 * kind + 8 * (j // 2) + 4 * (j % 2) + k
                plane[kind, k, j] = 96 * kind + 32 * k + j
    first = np.zeros((192, 256))
    second = np.zeros((256, 192))
    for a in range(2):
        for b in range(2):
            for k in range(3):
                first[np.ix_(plane[a, k], tile[b, k])] = step[a][b]
                second[np.ix_(tile[a, k], plane[b, k])] = step[a][b]
    return first.astype(np.float32), second.astype(np.float32)


def dot(a, b):
    return jnp.dot(a, b, preferred_element_type=f32)


def dot_nt(a, b):
    return lax.dot_general(a, b, (((1,), (1,)), ((), ())), preferred_element_type=f32)


def dot_tn(a, b):
    return lax.dot_general(a, b, (((0,), (0,)), ((), ())), preferred_element_type=f32)


def split2(x):
    high = x.astype(bf16)
    low = (x - high.astype(f32)).astype(bf16)
    return high, low


def split3(x):
    high = x.astype(bf16)
    rest = x - high.astype(f32)
    mid = rest.astype(bf16)
    low = (rest - mid.astype(f32)).astype(bf16)
    return high, mid, low


def parts3(x):
    high, mid, low = split3(x)
    return high.astype(f32), mid.astype(f32), low.astype(f32)


def moved_exactly(rows, hot, product):
    count = rows.shape[0]
    high, mid, low = split3(rows)
    out = product(jnp.concatenate([high, mid, low], axis=0), hot)
    return out[:count] + out[count : 2 * count] + out[2 * count :]


def rolled(x, shift):
    return pltpu.roll(x, shift, 1)


def bonds(planes, used_oxygen):
    one = [rolled(x, SLOTS - MOLS) for x in planes]
    two = [rolled(x, SLOTS - 2 * MOLS) for x in planes]
    d1 = [x - a for x, a in zip(planes, one)]
    d2 = [x - a for x, a in zip(planes, two)]
    d3 = [a - b for a, b in zip(one, two)]
    c1 = bond_stiffness * (d1[0] * d1[0] + d1[1] * d1[1] + d1[2] * d1[2] - bond_square)
    c2 = bond_stiffness * (d2[0] * d2[0] + d2[1] * d2[1] + d2[2] * d2[2] - bond_square)
    c3 = angle_stiffness * (d3[0] * d3[0] + d3[1] * d3[1] + d3[2] * d3[2] - angle_square)
    c1, c2, c3 = c1 * used_oxygen, c2 * used_oxygen, c3 * used_oxygen
    out = []
    for k in range(3):
        a, b, c = c1 * d1[k], c2 * d2[k], c3 * d3[k]
        out.append(rolled(a - c, MOLS) + rolled(b + c, 2 * MOLS) - (a + b))
    return out


def patterns():
    lane = lax.broadcasted_iota(jnp.int32, (1, SLOTS), 1)
    is_oxygen = jnp.where(lane < MOLS, 1.0, 0.0).astype(f32)
    charge = jnp.where(lane < MOLS, charge_oxygen, charge_hydrogen).astype(f32)
    return is_oxygen, charge


def left_features(xyz, row):
    norm = jnp.sum(xyz * xyz, axis=0, keepdims=True)
    full = jnp.where(row == 3, norm + coulomb_soft, jnp.where(row == 4, 1.0, xyz))
    h, m, l = parts3(full)
    return jnp.concatenate([h, h, m, m, h, l], axis=0).astype(bf16)


def right_features(xyz, row):
    norm = jnp.sum(xyz * xyz, axis=0, keepdims=True)
    full = jnp.where(row == 3, 1.0, jnp.where(row == 4, norm, -2.0 * xyz))
    h, m, l = parts3(full)
    return jnp.concatenate([h, m, h, m, l, h], axis=0).astype(bf16)


def sum_features(xyz, row, weight):
    full = jnp.where(row == 3, 1.0, xyz) * weight
    high = full.astype(bf16).astype(f32)
    return jnp.concatenate([high, full - high], axis=0).astype(bf16)


def both(high_low, feats, product):
    high, low = high_low
    out = product(feats, high) + product(feats, low)
    return out[0:8] + out[8:16]


def forces(tile_of, used_of, own_ref, next_ref, mask_ref, lj_mask_ref, first, last):
    is_oxygen, charge = patterns()
    row = lax.broadcasted_iota(jnp.int32, (8, SLOTS), 0)
    lane = lax.broadcasted_iota(jnp.int32, (8, SLOTS), 1)

    def xyz_of(tile, bead, shift):
        tile = tile if bead == 0 else pltpu.roll(tile, 4, 0)
        return jnp.where(row < 3, tile - jnp.where(row == 0, shift, 0.5), 0.0)

    def joined(parts):
        zero, one = parts
        return jnp.where(row < 4, zero, pltpu.roll(one, 4, 0))

    def strength(squares):
        y = lax.rsqrt(squares)
        return split2(y * y * y)

    def pulled(xyz, sums):
        return xyz * sums[3:4, :] - sums

    def beside(c, xyz, left, feats, q):
        tile, q2 = tile_of(c + 1), used_of(c + 1) * charge
        on_c, on_next = [], []
        for bead in range(2):
            xyz2 = xyz_of(tile, bead, -0.5)
            g = strength(dot_tn(left[bead], right_features(xyz2, row)))
            on_c.append(both(g, sum_features(xyz2, row, q2), dot_nt))
            on_next.append(pulled(xyz2, both(g, feats[bead], dot)))
        next_ref[c + 1] = joined(on_next) * (coulomb_scale * q2)
        return on_c

    def own(c, alone):
        tile, used = tile_of(c), used_of(c)
        q = used * charge
        xyz = [xyz_of(tile, bead, 0.5) for bead in range(2)]
        left = [left_features(x, row) for x in xyz]
        feats = [sum_features(x, row, q) for x in xyz]
        sums = beside(c, xyz, left, feats, q)
        if alone:
            return
        before, after = tile_of(c - 1), tile_of(c + 1)
        ox = used * is_oxygen
        ox_lanes = jnp.where(
            lane[:1] < MOLS,
            used_of(c - 1),
            jnp.where(
                lane[:1] < 2 * MOLS,
                rolled(used, MOLS),
                jnp.where(lane[:1] < 3 * MOLS, rolled(used_of(c + 1), 2 * MOLS), 0.0),
            ),
        )
        total = []
        for bead in range(2):
            squares = dot_tn(left[bead], right_features(xyz[bead], row)) + mask_ref[...]
            s = sums[bead] + both(strength(squares), feats[bead], dot)
            force = pulled(xyz[bead], s) * (coulomb_scale * q)
            three = jnp.where(
                lane < MOLS,
                xyz_of(before, bead, 1.5),
                jnp.where(
                    lane < 2 * MOLS,
                    rolled(xyz[bead], MOLS),
                    rolled(xyz_of(after, bead, -0.5), 2 * MOLS),
                ),
            )
            squares = dot_tn(left[bead][:, :48], right_features(three, row)) + lj_mask_ref[...]
            y = lax.rsqrt(squares + (lennard_soft - coulomb_soft))
            ratio = (sigma_square * y) * y
            cubed = ratio * ratio * ratio
            g = (2.0 * cubed * cubed - cubed) * (y * y * (24.0 * well_depth))
            t = both(split2(g), sum_features(three, row, ox_lanes), dot_nt)
            t = jnp.concatenate([t, jnp.zeros((8, SLOTS - 48), f32)], axis=1)
            total.append(force + pulled(xyz[bead], t) * ox)
        own_ref[c] = joined(total)

    own(first - 1, True)

    def body(c, carry):
        own(c, False)
        return carry

    lax.fori_loop(first, last + 1, body, 0)


def kernel(
    pos_ref,
    mom_ref,
    ids_ref,
    first_ref,
    second_ref,
    x_out,
    p_out,
    raw,
    hot,
    tiles,
    moms,
    own_ref,
    next_ref,
    mask_ref,
    lj_mask_ref,
    sent_v,
    mode_in,
    mode_out,
    back_x,
    back_v,
    halo_send,
    halo_recv,
    in_send,
    in_recv,
    out_send,
    out_recv,
    v_recv,
):
    b = lax.axis_index("bead")
    s = lax.axis_index("space")
    far = lax.rem(s + FLIP, SPACE)
    right = lax.rem(s + 1, SPACE)
    left = lax.rem(s + SPACE - 1, SPACE)
    far_right = lax.rem(far + 1, SPACE)
    far_left = lax.rem(far + SPACE - 1, SPACE)

    barrier = pltpu.get_barrier_semaphore()

    def hello(peer, carry):
        pl.semaphore_signal(barrier, inc=1, device_id=(peer, far), device_id_type=MESH)
        return carry

    lax.fori_loop(0, GROUP, hello, 0)
    for who in (
        (b, left),
        (b, right),
        (GROUP - 1, far_left),
        (0, far_right),
    ):
        pl.semaphore_signal(barrier, inc=1, device_id=who, device_id_type=MESH)

    raw[...] = jnp.zeros_like(raw)
    for bead in range(2):
        for k in range(3):
            raw[pl.ds(4 * bead + k, CELLS, stride=16), :] = pos_ref[bead, k]
            raw[pl.ds(8 + 4 * bead + k, CELLS, stride=16), :] = mom_ref[bead, k]

    sub = lax.broadcasted_iota(jnp.int32, (SLOTS, SLOTS), 0)
    lane = lax.broadcasted_iota(jnp.int32, (SLOTS, SLOTS), 1)
    same = (sub % MOLS == lane % MOLS) & (sub < 3 * MOLS) & (lane < 3 * MOLS)
    mask_ref[...] = jnp.where(same, BIG, 0.0).astype(f32)
    lj_mask_ref[...] = jnp.where(lane[:48] == sub[:48] + MOLS, BIG, 0.0).astype(f32)

    ids = ids_ref[...]
    used_all = jnp.where(ids < SLOTS, 1.0, 0.0).astype(f32)
    below = jnp.where(lane < sub, 1.0, 0.0).astype(bf16)
    above = jnp.where(sub < lane, 1.0, 0.0).astype(bf16)
    spare = dot((1.0 - used_all).astype(bf16), above)
    keys = jnp.where(ids < SLOTS, ids.astype(f32), spare + 1000.0)
    ones = jnp.ones((SLOTS, SLOTS), bf16)
    sub_f = sub.astype(f32)
    row16 = lax.broadcasted_iota(jnp.int32, (16, SLOTS), 0)

    for c in range(CELLS):
        key = keys[c : c + 1]
        used = used_all[c : c + 1]
        mine = sub_f == key
        taken = dot(jnp.where(mine, 1.0, 0.0).astype(bf16), ones)
        rank = sub_f - dot(below, taken.astype(bf16))
        spare_key = jnp.where(taken > 0.5, -1.0, rank + 1000.0)
        place = jnp.where(mine | (spare_key == key), 1.0, 0.0).astype(bf16)
        hot[c] = place
        rows = moved_exactly(raw[16 * c : 16 * c + 16], place, dot)
        rows = jnp.where(row16 == 3, used, rows)
        tiles[c + 1] = rows[:8]
        moms[c] = rows[8:]

    pl.semaphore_wait(
        barrier,
        GROUP + 2 + jnp.where(b == 0, GROUP, 0) + jnp.where(b == GROUP - 1, GROUP, 0),
    )

    to_left = pltpu.make_async_remote_copy(
        src_ref=tiles.at[1],
        dst_ref=tiles.at[CELLS + 1],
        send_sem=halo_send.at[0],
        recv_sem=halo_recv.at[0],
        device_id=(b, left),
        device_id_type=MESH,
    )
    to_right = pltpu.make_async_remote_copy(
        src_ref=tiles.at[CELLS],
        dst_ref=tiles.at[0],
        send_sem=halo_send.at[1],
        recv_sem=halo_recv.at[1],
        device_id=(b, right),
        device_id_type=MESH,
    )
    to_left.start()
    to_right.start()

    def send_x(i, carry):
        peer = lax.rem(b + GROUP // 2 + i, GROUP)
        pltpu.make_async_remote_copy(
            src_ref=tiles.at[peer + 1],
            dst_ref=mode_in.at[0, b],
            send_sem=in_send.at[0],
            recv_sem=in_recv.at[0],
            device_id=(peer, far),
            device_id_type=MESH,
        ).start()
        return carry

    lax.fori_loop(0, GROUP, send_x, 0)
    to_left.wait()
    to_right.wait()

    is_oxygen, _ = patterns()
    used_planes = jnp.concatenate([used_all, used_all], axis=0)
    used_ox = used_planes * is_oxygen
    inverse_mass = 1.0 - (15.0 / 16.0) * used_ox
    mass = 1.0 + 15.0 * used_ox

    def used_of(c):
        return tiles[c, 3:4, :]

    tiles_rows = tiles.reshape((CELLS + 2) * 8, SLOTS)
    moms_rows = moms.reshape(CELLS * 8, SLOTS)
    own_rows = own_ref.reshape((CELLS + 2) * 8, SLOTS)
    next_rows = next_ref.reshape((CELLS + 2) * 8, SLOTS)
    sent_rows = sent_v.reshape(CELLS * 8, SLOTS)
    back_x_rows = back_x.reshape((CELLS + 2) * 8, SLOTS)
    back_v_rows = back_v.reshape(CELLS * 8, SLOTS)

    def plane(ref, start, k):
        return jnp.concatenate(
            [ref[pl.ds(start + 4 * bead + k, CELLS, stride=8), :] for bead in range(2)], axis=0
        )

    forces(lambda c: tiles[c], used_of, own_ref, next_ref, mask_ref, lj_mask_ref, 1, CELLS)
    inner = bonds([plane(tiles_rows, 8, k) for k in range(3)], used_ox)
    sent_v[...] = jnp.zeros_like(sent_v)
    for k in range(3):
        outer = plane(own_rows, 8, k) + plane(next_rows, 8, k)
        p = plane(moms_rows, 0, k) + (0.5 * outer_step) * outer
        v = (p + (0.5 * inner_step) * inner[k]) * inverse_mass
        for bead in range(2):
            sent_rows[pl.ds(4 * bead + k, CELLS, stride=8), :] = v[CELLS * bead : CELLS * bead + CELLS]

    def send_v(i, carry):
        peer = lax.rem(b + GROUP // 2 + i, GROUP)
        pltpu.make_async_remote_copy(
            src_ref=sent_v.at[peer],
            dst_ref=mode_in.at[1, b],
            send_sem=in_send.at[1],
            recv_sem=in_recv.at[1],
            device_id=(peer, far),
            device_id_type=MESH,
        ).start()
        return carry

    lax.fori_loop(0, GROUP, send_v, 0)

    def all_of(kind, ref, send_sem, recv_sem):
        return pltpu.make_async_remote_copy(
            src_ref=ref,
            dst_ref=mode_in.at[kind],
            send_sem=send_sem,
            recv_sem=recv_sem,
            device_id=(b, far),
            device_id_type=MESH,
        )

    all_of(0, tiles.at[pl.ds(1, CELLS)], in_send.at[0], in_recv.at[0]).wait()
    all_of(1, sent_v, in_send.at[1], in_recv.at[1]).wait()

    mode_rows = mode_in[...].reshape(256, SLOTS)
    mode_ox = mode_in[0, 0, 3:4, :] * is_oxygen
    mode_inverse = 1.0 - (15.0 / 16.0) * mode_ox
    evolved = jnp.dot(first_ref[...], mode_rows, precision=lax.Precision.HIGHEST, preferred_element_type=f32)
    pull = bonds([evolved[32 * k : 32 * k + 32] for k in range(3)], mode_ox)
    kicked = [evolved[96 + 32 * k : 128 + 32 * k] + (inner_step * mode_inverse) * pull[k] for k in range(3)]
    state = jnp.concatenate([evolved[:96], *kicked], axis=0)
    mode_out[...] = jnp.dot(
        second_ref[...], state, precision=lax.Precision.HIGHEST, preferred_element_type=f32
    ).reshape(2, GROUP, 8, SLOTS)

    def back(kind, src, dst, group, recv_sem):
        def send(i, carry):
            peer = lax.rem(b + GROUP // 2 + i, GROUP)
            pltpu.make_async_remote_copy(
                src_ref=mode_out.at[kind, peer],
                dst_ref=dst,
                send_sem=out_send.at[src],
                recv_sem=recv_sem,
                device_id=(peer, group),
                device_id_type=MESH,
            ).start()
            return carry

        lax.fori_loop(0, GROUP, send, 0)

    back(0, 0, back_x.at[b + 1], far, out_recv.at[b + 1])

    @pl.when(b == 0)
    def _():
        back(0, 2, back_x.at[CELLS + 1], far_left, out_recv.at[CELLS + 1])

    @pl.when(b == GROUP - 1)
    def _():
        back(0, 2, back_x.at[0], far_right, out_recv.at[0])

    back(1, 1, back_v.at[b], far, v_recv)

    for c in range(CELLS + 2):
        pltpu.make_async_copy(back_x.at[c], back_x.at[c], out_recv.at[c]).wait()

    forces(lambda c: back_x[c], used_of, own_ref, next_ref, mask_ref, lj_mask_ref, 1, CELLS)
    inner = bonds([plane(back_x_rows, 8, k) for k in range(3)], used_ox)
    pltpu.make_async_copy(back_v, back_v, v_recv).wait()
    for k in range(3):
        outer = plane(own_rows, 8, k) + plane(next_rows, 8, k)
        p = mass * plane(back_v_rows, 0, k) + (0.5 * inner_step) * inner[k]
        p = p + (0.5 * outer_step) * outer
        x = plane(back_x_rows, 8, k)
        for bead in range(2):
            half = slice(CELLS * bead, CELLS * bead + CELLS)
            raw[pl.ds(4 * bead + k, CELLS, stride=16), :] = x[half]
            raw[pl.ds(8 + 4 * bead + k, CELLS, stride=16), :] = p[half]
    for c in range(CELLS):
        raw[16 * c : 16 * c + 16] = moved_exactly(raw[16 * c : 16 * c + 16], hot[c], dot_nt)
    for bead in range(2):
        for k in range(3):
            x_out[bead, k] = raw[pl.ds(4 * bead + k, CELLS, stride=16), :]
            p_out[bead, k] = raw[pl.ds(8 + 4 * bead + k, CELLS, stride=16), :]

    pltpu.make_async_copy(mode_out.at[0], mode_out.at[0], out_send.at[0]).wait()
    pltpu.make_async_copy(mode_out.at[1], mode_out.at[1], out_send.at[1]).wait()

    @pl.when((b == 0) | (b == GROUP - 1))
    def _():
        pltpu.make_async_copy(mode_out.at[0], mode_out.at[0], out_send.at[2]).wait()


def local(positions, momenta, molecules):
    ids = jnp.transpose(molecules, (0, 2, 1)).reshape(CELLS, 3 * MOLS)
    ids = jnp.pad(ids, ((0, 0), (0, SLOTS - 3 * MOLS)), constant_values=SLOTS)
    first, second = propagators()
    vmem = pl.BlockSpec(memory_space=pltpu.VMEM)
    return pl.pallas_call(
        kernel,
        out_shape=[jax.ShapeDtypeStruct(positions.shape, f32)] * 2,
        in_specs=[vmem] * 5,
        out_specs=[vmem] * 2,
        scratch_shapes=[
            pltpu.VMEM((CELLS * 16, SLOTS), f32),
            pltpu.VMEM((CELLS, SLOTS, SLOTS), bf16),
            pltpu.VMEM((CELLS + 2, 8, SLOTS), f32),
            pltpu.VMEM((CELLS, 8, SLOTS), f32),
            pltpu.VMEM((CELLS + 2, 8, SLOTS), f32),
            pltpu.VMEM((CELLS + 2, 8, SLOTS), f32),
            pltpu.VMEM((SLOTS, SLOTS), f32),
            pltpu.VMEM((48, SLOTS), f32),
            pltpu.VMEM((CELLS, 8, SLOTS), f32),
            pltpu.VMEM((2, GROUP, 8, SLOTS), f32),
            pltpu.VMEM((2, GROUP, 8, SLOTS), f32),
            pltpu.VMEM((CELLS + 2, 8, SLOTS), f32),
            pltpu.VMEM((CELLS, 8, SLOTS), f32),
            pltpu.SemaphoreType.DMA((2,)),
            pltpu.SemaphoreType.DMA((2,)),
            pltpu.SemaphoreType.DMA((2,)),
            pltpu.SemaphoreType.DMA((2,)),
            pltpu.SemaphoreType.DMA((3,)),
            pltpu.SemaphoreType.DMA((CELLS + 2,)),
            pltpu.SemaphoreType.DMA,
        ],
        compiler_params=pltpu.CompilerParams(collective_id=0, has_side_effects=True),
    )(positions, momenta, ids, jnp.asarray(first), jnp.asarray(second))


def solution(mesh):
    wide = P("bead", None, "space", None)
    return jax.shard_map(
        local,
        mesh=mesh,
        in_specs=(wide, wide, P("space", None, None)),
        out_specs=(wide, wide),
        check_vma=False,
    )
```

time: 157 us -> 75.6 us (0.48)
  Pallas kernels: 0 us -> 71.2 us
  starting transfers between devices: 52.1 us -> 0 us
  matrix products: 41.1 us -> 0 us
  other arithmetic: 29.3 us -> 0 us
  waiting for transfers between devices: 27.2 us -> 0 us
    pallas_call x0 -> x1, Pallas kernels: none -> 71.2 us  [local(): pl.pallas_call(kernel, out_shape=[jax.ShapeDtypeStruct(positions.shape, f...]
    dot_general x27 -> x0, matrix products: 41.1 us -> none  [the longest x12 35.2 us: pair_force(): jnp.einsum('nij,knj->kni', strength, peer_atoms, precision=lax.Precision....]
    ppermute x6 -> x0, starting transfers between devices: 29.4 us -> none  [the longest x3 23.7 us: padded(): lax.ppermute(head, axis, [((i + 1) % count, i) for i in range(count)])]
    all_to_all x2 -> x0, waiting for transfers between devices: 27.1 us -> none  [sent_together(): lax.all_to_all(both, axis, split_axis=split_dim, concat_axis=concat_dim,...]
    reduce_sum x17 -> x0, other arithmetic: 26.8 us -> none  [the longest x12 26.1 us: pair_force(): totals = jnp.sum(strength, axis=2)]
    all_to_all x2 -> x0, starting transfers between devices: 22.7 us -> none  [sent_together(): lax.all_to_all(both, axis, split_axis=split_dim, concat_axis=concat_dim,...]
    slice x28 -> x0, local copies, waits for them, and re-layouts: 2.01 us -> none  [the longest x3 1.51 us: padded(): lax.slice_in_dim(cells, cells.shape[dim] - width, cells.shape[dim], axis=...]
  transfers between devices with their start and end apart: 8 -> 0, of which waited for: 2 -> 0; matrix products, arithmetic and copies ran while one was open for 14% -> 0% of each run, Pallas kernels for 0% -> 0%
where the time goes in v1:
time: 75.6 us; the launch traced here: 75.4 us
  Pallas kernels  71.2 us (94%)
  local copies, waits for them, and re-layouts  3.5 us (5%)
    pallas_call x1, Pallas kernels, local(): pl.pallas_call(kernel, out_shape=[jax.ShapeDtypeStruct(positions.shape, f...  71.2 us
    unnamed x4, local copies, waits for them, and re-layouts  2.06 us

profile of v1, /device:TPU:2, one launch (start us, length us, event | category | flops | bytes accessed | tf_op | source)
XLA Modules:
  0.0 75.4 jit_solution(2380833359316662161)
XLA Ops:
  0.6 0.8 copy.8
  1.4 0.1 reshape.7
  1.5 0.6 pad.4.ids_ref
  2.1 71.2 %shard_map.68 = (f32[2,3,16,128]{3,2,1,0:T(8,128)}, f32[2,3,16,128]{3,2,1,0:T(8,128)}) custom-call(f32[2,3,16,128]{3,2,1,0:T(8,128)} %pos_ref.1, f32[2,3,16,128]{3,2,1,0:T(8,128)} %mom_ref.1, s32[16,128]{1,0:T(8,128)} %pad.4.ids_ref, f32[192,256]{1,0:T(8,128)} %constant.6.clone.first_ref, f32[256,192]{1,0:T(8,128)} %constant.7.clone.second_ref), custom_call_target="tpu_custom_call" | custom-call | tf_op jit(solution)/shard_map/pallas_call | solution.py:518
  73.3 0.0 copy-start
  73.3 1.4 %copy.11 = f32[2,3,16,128]{3,2,1,0:T(8,128)} copy(f32[2,3,16,128]{3,2,1,0:T(8,128)} %get-tuple-element.4) | data formatting | bytes 98304
  74.8 0.0 copy-done
  74.8 0.6 copy.12
Async XLA Ops:
  73.3 1.4 %copy-start = (f32[2,3,16,128]{3,2,1,0:T(8,128)S(1)}, f32[2,3,16,128]{3,2,1,0:T(8,128)}, u32[]{:S(2)}) copy-start(f32[2,3,16,128]{3,2,1,0:T(8,128)} %get-tuple-element.5) | copy-start | bytes 147460

commit v2 on v1

--- a/solution.py
+++ b/solution.py
@@ -87,10 +87,6 @@
     return lax.dot_general(a, b, (((1,), (1,)), ((), ())), preferred_element_type=f32)
 
 
-def dot_tn(a, b):
-    return lax.dot_general(a, b, (((0,), (0,)), ((), ())), preferred_element_type=f32)
-
-
 def split2(x):
     high = x.astype(bf16)
     low = (x - high.astype(f32)).astype(bf16)
@@ -145,114 +141,149 @@
     return is_oxygen, charge
 
 
-def left_features(xyz, row):
-    norm = jnp.sum(xyz * xyz, axis=0, keepdims=True)
-    full = jnp.where(row == 3, norm + coulomb_soft, jnp.where(row == 4, 1.0, xyz))
+def bead_rows(bead):
+    row = lax.broadcasted_iota(jnp.int32, (8, SLOTS), 0)
+    return (row >= 4 * bead) & (row < 4 * bead + 3), row == 4 * bead + 3, row == (4 * bead + 4) % 8
+
+
+def left_features(xyz, norm, rows):
+    _, is_norm, is_one = rows
+    full = jnp.where(is_norm, norm + coulomb_soft, jnp.where(is_one, 1.0, xyz))
     h, m, l = parts3(full)
     return jnp.concatenate([h, h, m, m, h, l], axis=0).astype(bf16)
 
 
-def right_features(xyz, row):
-    norm = jnp.sum(xyz * xyz, axis=0, keepdims=True)
-    full = jnp.where(row == 3, 1.0, jnp.where(row == 4, norm, -2.0 * xyz))
+def right_features(xyz, norm, rows):
+    _, is_norm, is_one = rows
+    full = jnp.where(is_norm, 1.0, jnp.where(is_one, norm, -2.0 * xyz))
     h, m, l = parts3(full)
     return jnp.concatenate([h, m, h, m, l, h], axis=0).astype(bf16)
 
 
-def sum_features(xyz, row, weight):
-    full = jnp.where(row == 3, 1.0, xyz) * weight
+def sum_features(xyz, rows, weight):
+    full = jnp.where(rows[1], 1.0, xyz) * weight
     high = full.astype(bf16).astype(f32)
     return jnp.concatenate([high, full - high], axis=0).astype(bf16)
 
 
-def both(high_low, feats, product):
-    high, low = high_low
-    out = product(feats, high) + product(feats, low)
+def squared(xyz):
+    return jnp.sum(xyz * xyz, axis=0, keepdims=True)
+
+
+def pulled(xyz, sums, bead):
+    return xyz * sums[4 * bead + 3 : 4 * bead + 4, :] - sums
+
+
+def folded(out):
     return out[0:8] + out[8:16]
 
 
-def forces(tile_of, used_of, own_ref, next_ref, mask_ref, lj_mask_ref, first, last):
-    is_oxygen, charge = patterns()
-    row = lax.broadcasted_iota(jnp.int32, (8, SLOTS), 0)
-    lane = lax.broadcasted_iota(jnp.int32, (8, SLOTS), 1)
-
-    def xyz_of(tile, bead, shift):
-        tile = tile if bead == 0 else pltpu.roll(tile, 4, 0)
-        return jnp.where(row < 3, tile - jnp.where(row == 0, shift, 0.5), 0.0)
-
-    def joined(parts):
-        zero, one = parts
-        return jnp.where(row < 4, zero, pltpu.roll(one, 4, 0))
-
-    def strength(squares):
-        y = lax.rsqrt(squares)
-        return split2(y * y * y)
-
-    def pulled(xyz, sums):
-        return xyz * sums[3:4, :] - sums
-
-    def beside(c, xyz, left, feats, q):
-        tile, q2 = tile_of(c + 1), used_of(c + 1) * charge
-        on_c, on_next = [], []
-        for bead in range(2):
-            xyz2 = xyz_of(tile, bead, -0.5)
-            g = strength(dot_tn(left[bead], right_features(xyz2, row)))
-            on_c.append(both(g, sum_features(xyz2, row, q2), dot_nt))
-            on_next.append(pulled(xyz2, both(g, feats[bead], dot)))
-        next_ref[c + 1] = joined(on_next) * (coulomb_scale * q2)
-        return on_c
-
-    def own(c, alone):
-        tile, used = tile_of(c), used_of(c)
-        q = used * charge
-        xyz = [xyz_of(tile, bead, 0.5) for bead in range(2)]
-        left = [left_features(x, row) for x in xyz]
-        feats = [sum_features(x, row, q) for x in xyz]
-        sums = beside(c, xyz, left, feats, q)
+CHUNK = 32
+
+
+class Forces:
+    def __init__(self, tile_of, used_of, own_ref, next_ref, mask_ref, lj_mask_ref, near_ref, ox_ref, feats_ref, ox_feats_ref):
+        self.tile_of, self.used_of, self.own_ref, self.next_ref = tile_of, used_of, own_ref, next_ref
+        self.mask_ref, self.lj_mask_ref, self.near_ref, self.ox_ref = mask_ref, lj_mask_ref, near_ref, ox_ref
+        self.feats_ref, self.ox_feats_ref = feats_ref, ox_feats_ref
+        self.is_oxygen, self.charge = patterns()
+        self.rows = [bead_rows(bead) for bead in range(2)]
+        self.row = lax.broadcasted_iota(jnp.int32, (8, SLOTS), 0)
+        self.lane = lax.broadcasted_iota(jnp.int32, (8, SLOTS), 1)
+
+    def xyz(self, c, bead, cell_shift):
+        shift = jnp.where(self.row == 4 * bead, 0.5 - cell_shift, 0.5)
+        return jnp.where(self.rows[bead][0], self.tile_of(c) - shift, 0.0)
+
+    def squares(self, c, bead, alone=False):
+        rows, lane = self.rows[bead], self.lane
+        used, used2 = self.used_of(c), self.used_of(c + 1)
+        xyz, xyz2 = self.xyz(c, bead, 0.0), self.xyz(c + 1, bead, 1.0)
+        norm, norm2 = squared(xyz), squared(xyz2)
+        left = left_features(xyz, norm, rows).T
+        right2 = right_features(xyz2, norm2, rows)
+        feats = sum_features(xyz, rows, used * self.charge)
+        feats2 = sum_features(xyz2, rows, used2 * self.charge)
+        self.feats_ref[bead] = jnp.concatenate([feats, feats2], axis=1)
         if alone:
+            self.near_ref[bead, :, SLOTS:] = dot(left, right2)
             return
-        before, after = tile_of(c - 1), tile_of(c + 1)
-        ox = used * is_oxygen
-        ox_lanes = jnp.where(
+        right = jnp.concatenate([right_features(xyz, norm, rows), right2], axis=1)
+        self.near_ref[bead] = dot(left, right)
+        used0, xyz0 = self.used_of(c - 1), self.xyz(c - 1, bead, -1.0)
+        three = jnp.where(
+            lane < MOLS,
+            xyz0,
+            jnp.where(lane < 2 * MOLS, rolled(xyz, MOLS), rolled(xyz2, 2 * MOLS)),
+        )
+        ox = jnp.where(
             lane[:1] < MOLS,
-            used_of(c - 1),
+            used0,
             jnp.where(
                 lane[:1] < 2 * MOLS,
                 rolled(used, MOLS),
-                jnp.where(lane[:1] < 3 * MOLS, rolled(used_of(c + 1), 2 * MOLS), 0.0),
+                jnp.where(lane[:1] < 3 * MOLS, rolled(used2, 2 * MOLS), 0.0),
             ),
         )
-        total = []
+        right = right_features(three, squared(three) + (lennard_soft - coulomb_soft), rows)
+        self.ox_ref[bead] = dot(left[:48], right)
+        self.ox_feats_ref[bead] = sum_features(three, rows, ox)
+
+    def next_sums(self, c, bead, g):
+        xyz2 = self.xyz(c + 1, bead, 1.0)
+        feats = self.feats_ref[bead, :, :SLOTS]
+        sums = folded(dot(feats, g[0]) + dot(feats, g[1]))
+        return pulled(xyz2, sums, bead) * (coulomb_scale * self.used_of(c + 1) * self.charge)
+
+    def sums(self, c, bead):
+        high, low = [], []
+        for i in range(0, SLOTS, CHUNK):
+            part = self.near_ref[bead, i : i + CHUNK]
+            part = jnp.concatenate([part[:, :SLOTS] + self.mask_ref[i : i + CHUNK], part[:, SLOTS:]], axis=1)
+            y = lax.rsqrt(part)
+            h, l = split2(y * y * y)
+            high.append(h)
+            low.append(l)
+        high, low = jnp.concatenate(high, axis=0), jnp.concatenate(low, axis=0)
+        y = lax.rsqrt(self.ox_ref[bead] + self.lj_mask_ref[...])
+        inverse = y * y
+        cubed = (inverse * inverse) * (inverse * sigma_square**3)
+        g = cubed * (cubed * (48.0 * well_depth) - 24.0 * well_depth) * inverse
+        ox_high, ox_low = split2(g)
+        xyz = self.xyz(c, bead, 0.0)
+        used = self.used_of(c)
+        feats = self.feats_ref[bead]
+        near = folded(dot_nt(feats, high) + dot_nt(feats, low))
+        after = self.next_sums(c, bead, (high[:, SLOTS:], low[:, SLOTS:]))
+        ox_feats = self.ox_feats_ref[bead]
+        ox = folded(dot_nt(ox_feats, ox_high) + dot_nt(ox_feats, ox_low))
+        ox = jnp.concatenate([ox, jnp.zeros((8, SLOTS - 48), f32)], axis=1)
+        force = pulled(xyz, near, bead) * (coulomb_scale * used * self.charge)
+        return force + pulled(xyz, ox, bead) * (used * self.is_oxygen), after
+
+    def first_halo(self):
+        out = []
         for bead in range(2):
-            squares = dot_tn(left[bead], right_features(xyz[bead], row)) + mask_ref[...]
-            s = sums[bead] + both(strength(squares), feats[bead], dot)
-            force = pulled(xyz[bead], s) * (coulomb_scale * q)
-            three = jnp.where(
-                lane < MOLS,
-                xyz_of(before, bead, 1.5),
-                jnp.where(
-                    lane < 2 * MOLS,
-                    rolled(xyz[bead], MOLS),
-                    rolled(xyz_of(after, bead, -0.5), 2 * MOLS),
-                ),
-            )
-            squares = dot_tn(left[bead][:, :48], right_features(three, row)) + lj_mask_ref[...]
-            y = lax.rsqrt(squares + (lennard_soft - coulomb_soft))
-            ratio = (sigma_square * y) * y
-            cubed = ratio * ratio * ratio
-            g = (2.0 * cubed * cubed - cubed) * (y * y * (24.0 * well_depth))
-            t = both(split2(g), sum_features(three, row, ox_lanes), dot_nt)
-            t = jnp.concatenate([t, jnp.zeros((8, SLOTS - 48), f32)], axis=1)
-            total.append(force + pulled(xyz[bead], t) * ox)
-        own_ref[c] = joined(total)
-
-    own(first - 1, True)
-
-    def body(c, carry):
-        own(c, False)
-        return carry
-
-    lax.fori_loop(first, last + 1, body, 0)
+            self.squares(0, bead, alone=True)
+        for bead in range(2):
+            y = lax.rsqrt(self.near_ref[bead, :, SLOTS:])
+            out.append(self.next_sums(0, bead, split2(y * y * y)))
+        self.next_ref[1] = jnp.where(self.row < 4, out[0], out[1])
+
+    def cells(self, cell_of, count):
+        self.squares(cell_of(0), 0)
+
+        def body(i, carry):
+            c = cell_of(i)
+            self.squares(c, 1)
+            near0, after0 = self.sums(c, 0)
+            self.squares(cell_of(jnp.minimum(i + 1, count - 1)), 0)
+            near1, after1 = self.sums(c, 1)
+            self.own_ref[c] = jnp.where(self.row < 4, near0, near1)
+            self.next_ref[c + 1] = jnp.where(self.row < 4, after0, after1)
+            return carry
+
+        lax.fori_loop(0, count, body, 0)
 
 
 def kernel(
@@ -271,6 +302,10 @@
     next_ref,
     mask_ref,
     lj_mask_ref,
+    near_ref,
+    ox_ref,
+    feats_ref,
+    ox_feats_ref,
     sent_v,
     mode_in,
     mode_out,
@@ -380,8 +415,6 @@
         return carry
 
     lax.fori_loop(0, GROUP, send_x, 0)
-    to_left.wait()
-    to_right.wait()
 
     is_oxygen, _ = patterns()
     used_planes = jnp.concatenate([used_all, used_all], axis=0)
@@ -405,7 +438,13 @@
             [ref[pl.ds(start + 4 * bead + k, CELLS, stride=8), :] for bead in range(2)], axis=0
         )
 
-    forces(lambda c: tiles[c], used_of, own_ref, next_ref, mask_ref, lj_mask_ref, 1, CELLS)
+    scratch = (own_ref, next_ref, mask_ref, lj_mask_ref, near_ref, ox_ref, feats_ref, ox_feats_ref)
+    now = Forces(lambda c: tiles[c], used_of, *scratch)
+    now.cells(lambda i: i + 2, CELLS - 2)
+    to_left.wait()
+    to_right.wait()
+    now.cells(lambda i: CELLS - (CELLS - 1) * i, 2)
+    now.first_halo()
     inner = bonds([plane(tiles_rows, 8, k) for k in range(3)], used_ox)
     sent_v[...] = jnp.zeros_like(sent_v)
     for k in range(3):
@@ -483,7 +522,9 @@
     for c in range(CELLS + 2):
         pltpu.make_async_copy(back_x.at[c], back_x.at[c], out_recv.at[c]).wait()
 
-    forces(lambda c: back_x[c], used_of, own_ref, next_ref, mask_ref, lj_mask_ref, 1, CELLS)
+    then = Forces(lambda c: back_x[c], used_of, *scratch)
+    then.cells(lambda i: i + 1, CELLS)
+    then.first_halo()
     inner = bonds([plane(back_x_rows, 8, k) for k in range(3)], used_ox)
     pltpu.make_async_copy(back_v, back_v, v_recv).wait()
     for k in range(3):
@@ -529,6 +570,10 @@
             pltpu.VMEM((CELLS + 2, 8, SLOTS), f32),
             pltpu.VMEM((SLOTS, SLOTS), f32),
             pltpu.VMEM((48, SLOTS), f32),
+            pltpu.VMEM((2, SLOTS, 2 * SLOTS), f32),
+            pltpu.VMEM((2, 48, SLOTS), f32),
+            pltpu.VMEM((2, 16, 2 * SLOTS), bf16),
+            pltpu.VMEM((2, 16, SLOTS), bf16),
             pltpu.VMEM((CELLS, 8, SLOTS), f32),
             pltpu.VMEM((2, GROUP, 8, SLOTS), f32),
             pltpu.VMEM((2, GROUP, 8, SLOTS), f32),

time: 75.6 us -> 55.3 us (0.73)
  Pallas kernels: 71.2 us -> 50.9 us
    pallas_call x1, Pallas kernels: 71.2 us -> 50.9 us  [local(): pl.pallas_call(kernel, out_shape=[jax.ShapeDtypeStruct(positions.shape, f...]
where the time goes in v2:
time: 55.3 us; the launch traced here: 55 us
  Pallas kernels  50.9 us (92%)
  local copies, waits for them, and re-layouts  3.5 us (6%)
  between operations  0.65 us (1%)
    pallas_call x1, Pallas kernels, local(): pl.pallas_call(kernel, out_shape=[jax.ShapeDtypeStruct(positions.shape, f...  50.9 us
    unnamed x4, local copies, waits for them, and re-layouts  2.06 us

profile of v2, /device:TPU:2, one launch (start us, length us, event | category | flops | bytes accessed | tf_op | source)
XLA Modules:
  0.0 55.0 jit_solution(2264465992701032161)
XLA Ops:
  0.6 0.8 %copy.8 = s32[16,3,42]{2,1,0:T(4,128)S(1)} copy(s32[16,3,42]{2,0,1:T(8,128)} %bitcast.1) | data formatting | bytes 16128 | tf_op jit(solution)/shard_map/transpose | solution.py:555
  1.4 0.1 reshape.7
  1.5 0.6 %pad.4.ids_ref = s32[16,128]{1,0:T(8,128)} pad(s32[16,126]{1,0:T(8,128)S(1)} %reshape.7, s32[]{:T(128)} %constant.2.clone.1), padding=0_0x0_2 | pad | bytes 16260 | tf_op jit(solution)/shard_map/jit(_pad)/pad | solution.py:556
  2.1 50.9 %shard_map.68 = (f32[2,3,16,128]{3,2,1,0:T(8,128)}, f32[2,3,16,128]{3,2,1,0:T(8,128)}) custom-call(f32[2,3,16,128]{3,2,1,0:T(8,128)} %pos_ref.1, f32[2,3,16,128]{3,2,1,0:T(8,128)} %mom_ref.1, s32[16,128]{1,0:T(8,128)} %pad.4.ids_ref, f32[192,256]{1,0:T(8,128)} %constant.6.clone.first_ref, f32[256,192]{1,0:T(8,128)} %constant.7.clone.second_ref), custom_call_target="tpu_custom_call" | custom-call | tf_op jit(solution)/shard_map/pallas_call | solution.py:559
  53.0 0.0 copy-start
  53.0 1.4 %copy.11 = f32[2,3,16,128]{3,2,1,0:T(8,128)} copy(f32[2,3,16,128]{3,2,1,0:T(8,128)} %get-tuple-element.4) | data formatting | bytes 98304
  54.4 0.0 copy-done
  54.4 0.6 %copy.12 = f32[2,3,16,128]{3,2,1,0:T(8,128)} copy(f32[2,3,16,128]{3,2,1,0:T(8,128)S(1)} %copy-done) | data formatting | bytes 98304
Async XLA Ops:
  53.0 1.4 %copy-start = (f32[2,3,16,128]{3,2,1,0:T(8,128)S(1)}, f32[2,3,16,128]{3,2,1,0:T(8,128)}, u32[]{:S(2)}) copy-start(f32[2,3,16,128]{3,2,1,0:T(8,128)} %get-tuple-element.5) | copy-start | bytes 147460

commit v3 on v2

--- a/solution.py
+++ b/solution.py
@@ -79,6 +79,10 @@
     return first.astype(np.float32), second.astype(np.float32)
 
 
+def thirds(matrix):
+    return jnp.stack(split3(jnp.asarray(matrix)))
+
+
 def dot(a, b):
     return jnp.dot(a, b, preferred_element_type=f32)
 
@@ -111,6 +115,14 @@
     high, mid, low = split3(rows)
     out = product(jnp.concatenate([high, mid, low], axis=0), hot)
     return out[:count] + out[count : 2 * count] + out[2 * count :]
+
+
+def by_thirds(matrix_ref, x):
+    high, mid, low = split3(x)
+    both = jnp.concatenate([high, mid], axis=1)
+    out = dot(matrix_ref[0], both) + dot(matrix_ref[1], both)
+    small = dot(matrix_ref[0], low) + dot(matrix_ref[2], high)
+    return out[:, :SLOTS] + (out[:, SLOTS:] + small)
 
 
 def rolled(x, shift):
@@ -271,19 +283,21 @@
         self.next_ref[1] = jnp.where(self.row < 4, out[0], out[1])
 
     def cells(self, cell_of, count):
-        self.squares(cell_of(0), 0)
+        for bead in range(2):
+            self.squares(cell_of(0), bead)
 
         def body(i, carry):
             c = cell_of(i)
-            self.squares(c, 1)
+            follows = cell_of(jnp.minimum(i + 1, count - 1))
             near0, after0 = self.sums(c, 0)
-            self.squares(cell_of(jnp.minimum(i + 1, count - 1)), 0)
+            self.squares(follows, 0)
             near1, after1 = self.sums(c, 1)
+            self.squares(follows, 1)
             self.own_ref[c] = jnp.where(self.row < 4, near0, near1)
             self.next_ref[c + 1] = jnp.where(self.row < 4, after0, after1)
             return carry
 
-        lax.fori_loop(0, count, body, 0)
+        lax.fori_loop(0, count, body, 0, unroll=2)
 
 
 def kernel(
@@ -324,8 +338,12 @@
     far = lax.rem(s + FLIP, SPACE)
     right = lax.rem(s + 1, SPACE)
     left = lax.rem(s + SPACE - 1, SPACE)
-    far_right = lax.rem(far + 1, SPACE)
-    far_left = lax.rem(far + SPACE - 1, SPACE)
+    x_own, z_own = b // 4, lax.rem(b, 4)
+    late = z_own >= 2
+    z_far = z_own + jnp.where(s < SPACE // 2, 1, 2)
+
+    def far_first(i):
+        return lax.rem(x_own + 2 + lax.rem(i, 4), 4) * 4 + lax.rem(z_far + i // 4, 4)
 
     barrier = pltpu.get_barrier_semaphore()
 
@@ -334,13 +352,8 @@
         return carry
 
     lax.fori_loop(0, GROUP, hello, 0)
-    for who in (
-        (b, left),
-        (b, right),
-        (GROUP - 1, far_left),
-        (0, far_right),
-    ):
-        pl.semaphore_signal(barrier, inc=1, device_id=who, device_id_type=MESH)
+    for who in (left, right):
+        pl.semaphore_signal(barrier, inc=1, device_id=(b, who), device_id_type=MESH)
 
     raw[...] = jnp.zeros_like(raw)
     for bead in range(2):
@@ -354,9 +367,13 @@
     mask_ref[...] = jnp.where(same, BIG, 0.0).astype(f32)
     lj_mask_ref[...] = jnp.where(lane[:48] == sub[:48] + MOLS, BIG, 0.0).astype(f32)
 
-    ids = ids_ref[...]
+    ids = jnp.full((CELLS, SLOTS), SLOTS, jnp.int32)
+    lane16 = lane[:CELLS]
+    for t in range(3):
+        padded = jnp.concatenate([ids_ref[t], jnp.zeros((CELLS, SLOTS - MOLS), jnp.int32)], axis=1)
+        here = (lane16 >= t * MOLS) & (lane16 < (t + 1) * MOLS)
+        ids = jnp.where(here, padded if t == 0 else rolled(padded, t * MOLS), ids)
     used_all = jnp.where(ids < SLOTS, 1.0, 0.0).astype(f32)
-    below = jnp.where(lane < sub, 1.0, 0.0).astype(bf16)
     above = jnp.where(sub < lane, 1.0, 0.0).astype(bf16)
     spare = dot((1.0 - used_all).astype(bf16), above)
     keys = jnp.where(ids < SLOTS, ids.astype(f32), spare + 1000.0)
@@ -364,57 +381,65 @@
     sub_f = sub.astype(f32)
     row16 = lax.broadcasted_iota(jnp.int32, (16, SLOTS), 0)
 
+    def taken_below(c):
+        key = keys[c : c + 1]
+        return dot(jnp.where(key < sub_f, 1.0, jnp.where(key == sub_f, 0.5, 0.0)).astype(bf16), ones)
+
+    ahead = [taken_below(c) for c in range(2)]
     for c in range(CELLS):
+        if c + 2 < CELLS:
+            ahead.append(taken_below(c + 2))
         key = keys[c : c + 1]
-        used = used_all[c : c + 1]
-        mine = sub_f == key
-        taken = dot(jnp.where(mine, 1.0, 0.0).astype(bf16), ones)
-        rank = sub_f - dot(below, taken.astype(bf16))
-        spare_key = jnp.where(taken > 0.5, -1.0, rank + 1000.0)
-        place = jnp.where(mine | (spare_key == key), 1.0, 0.0).astype(bf16)
+        spare_key = (sub_f + 1000.0) - ahead[c]
+        place = jnp.where((sub_f == key) | (spare_key == key), 1.0, 0.0).astype(bf16)
         hot[c] = place
         rows = moved_exactly(raw[16 * c : 16 * c + 16], place, dot)
-        rows = jnp.where(row16 == 3, used, rows)
+        rows = jnp.where(row16 == 3, used_all[c : c + 1], rows)
         tiles[c + 1] = rows[:8]
         moms[c] = rows[8:]
 
-    pl.semaphore_wait(
-        barrier,
-        GROUP + 2 + jnp.where(b == 0, GROUP, 0) + jnp.where(b == GROUP - 1, GROUP, 0),
-    )
-
-    to_left = pltpu.make_async_remote_copy(
-        src_ref=tiles.at[1],
-        dst_ref=tiles.at[CELLS + 1],
-        send_sem=halo_send.at[0],
-        recv_sem=halo_recv.at[0],
-        device_id=(b, left),
-        device_id_type=MESH,
-    )
-    to_right = pltpu.make_async_remote_copy(
-        src_ref=tiles.at[CELLS],
-        dst_ref=tiles.at[0],
-        send_sem=halo_send.at[1],
-        recv_sem=halo_recv.at[1],
-        device_id=(b, right),
-        device_id_type=MESH,
-    )
-    to_left.start()
-    to_right.start()
-
-    def send_x(i, carry):
-        peer = lax.rem(b + GROUP // 2 + i, GROUP)
-        pltpu.make_async_remote_copy(
-            src_ref=tiles.at[peer + 1],
-            dst_ref=mode_in.at[0, b],
-            send_sem=in_send.at[0],
-            recv_sem=in_recv.at[0],
-            device_id=(peer, far),
-            device_id_type=MESH,
-        ).start()
-        return carry
-
-    lax.fori_loop(0, GROUP, send_x, 0)
+    def beside(first, last, below, above, at):
+        return [
+            pltpu.make_async_remote_copy(
+                src_ref=first,
+                dst_ref=above,
+                send_sem=halo_send.at[at],
+                recv_sem=halo_recv.at[at],
+                device_id=(b, left),
+                device_id_type=MESH,
+            ),
+            pltpu.make_async_remote_copy(
+                src_ref=last,
+                dst_ref=below,
+                send_sem=halo_send.at[at + 1],
+                recv_sem=halo_recv.at[at + 1],
+                device_id=(b, right),
+                device_id_type=MESH,
+            ),
+        ]
+
+    def send_in(kind, ref, first):
+        def send(i, carry):
+            peer = far_first(i)
+            pltpu.make_async_remote_copy(
+                src_ref=ref.at[peer + first],
+                dst_ref=mode_in.at[kind, b],
+                send_sem=in_send.at[kind],
+                recv_sem=in_recv.at[kind],
+                device_id=(peer, far),
+                device_id_type=MESH,
+            ).start()
+            return carry
+
+        lax.fori_loop(0, GROUP, send, 0)
+
+    halos = beside(tiles.at[1], tiles.at[CELLS], tiles.at[0], tiles.at[CELLS + 1], 0)
+
+    def greet():
+        pl.semaphore_wait(barrier, GROUP + 2)
+        for copy in halos:
+            copy.start()
+        send_in(0, tiles, 1)
 
     is_oxygen, _ = patterns()
     used_planes = jnp.concatenate([used_all, used_all], axis=0)
@@ -440,9 +465,12 @@
 
     scratch = (own_ref, next_ref, mask_ref, lj_mask_ref, near_ref, ox_ref, feats_ref, ox_feats_ref)
     now = Forces(lambda c: tiles[c], used_of, *scratch)
-    now.cells(lambda i: i + 2, CELLS - 2)
-    to_left.wait()
-    to_right.wait()
+    now.cells(lambda i: i + 2, 4)
+    pl.when(late)(greet)
+    now.cells(lambda i: i + 6, CELLS - 6)
+    pl.when(jnp.logical_not(late))(greet)
+    for copy in halos:
+        copy.wait()
     now.cells(lambda i: CELLS - (CELLS - 1) * i, 2)
     now.first_halo()
     inner = bonds([plane(tiles_rows, 8, k) for k in range(3)], used_ox)
@@ -454,19 +482,7 @@
         for bead in range(2):
             sent_rows[pl.ds(4 * bead + k, CELLS, stride=8), :] = v[CELLS * bead : CELLS * bead + CELLS]
 
-    def send_v(i, carry):
-        peer = lax.rem(b + GROUP // 2 + i, GROUP)
-        pltpu.make_async_remote_copy(
-            src_ref=sent_v.at[peer],
-            dst_ref=mode_in.at[1, b],
-            send_sem=in_send.at[1],
-            recv_sem=in_recv.at[1],
-            device_id=(peer, far),
-            device_id_type=MESH,
-        ).start()
-        return carry
-
-    lax.fori_loop(0, GROUP, send_v, 0)
+    send_in(1, sent_v, 0)
 
     def all_of(kind, ref, send_sem, recv_sem):
         return pltpu.make_async_remote_copy(
@@ -484,46 +500,45 @@
     mode_rows = mode_in[...].reshape(256, SLOTS)
     mode_ox = mode_in[0, 0, 3:4, :] * is_oxygen
     mode_inverse = 1.0 - (15.0 / 16.0) * mode_ox
-    evolved = jnp.dot(first_ref[...], mode_rows, precision=lax.Precision.HIGHEST, preferred_element_type=f32)
+    evolved = by_thirds(first_ref, mode_rows)
     pull = bonds([evolved[32 * k : 32 * k + 32] for k in range(3)], mode_ox)
     kicked = [evolved[96 + 32 * k : 128 + 32 * k] + (inner_step * mode_inverse) * pull[k] for k in range(3)]
     state = jnp.concatenate([evolved[:96], *kicked], axis=0)
-    mode_out[...] = jnp.dot(
-        second_ref[...], state, precision=lax.Precision.HIGHEST, preferred_element_type=f32
-    ).reshape(2, GROUP, 8, SLOTS)
-
-    def back(kind, src, dst, group, recv_sem):
+    mode_out[...] = by_thirds(second_ref, state).reshape(2, GROUP, 8, SLOTS)
+
+    def back(kind, dst, recv_sem):
         def send(i, carry):
-            peer = lax.rem(b + GROUP // 2 + i, GROUP)
+            peer = far_first(i)
             pltpu.make_async_remote_copy(
                 src_ref=mode_out.at[kind, peer],
                 dst_ref=dst,
-                send_sem=out_send.at[src],
+                send_sem=out_send.at[kind],
                 recv_sem=recv_sem,
-                device_id=(peer, group),
+                device_id=(peer, far),
                 device_id_type=MESH,
             ).start()
             return carry
 
         lax.fori_loop(0, GROUP, send, 0)
 
-    back(0, 0, back_x.at[b + 1], far, out_recv.at[b + 1])
-
-    @pl.when(b == 0)
-    def _():
-        back(0, 2, back_x.at[CELLS + 1], far_left, out_recv.at[CELLS + 1])
-
-    @pl.when(b == GROUP - 1)
-    def _():
-        back(0, 2, back_x.at[0], far_right, out_recv.at[0])
-
-    back(1, 1, back_v.at[b], far, v_recv)
-
-    for c in range(CELLS + 2):
+    back(0, back_x.at[b + 1], out_recv.at[b + 1])
+    back(1, back_v.at[b], v_recv)
+
+    def arrived(c):
         pltpu.make_async_copy(back_x.at[c], back_x.at[c], out_recv.at[c]).wait()
 
+    halos = beside(back_x.at[1], back_x.at[CELLS], back_x.at[0], back_x.at[CELLS + 1], 2)
+    for c, copy in ((1, halos[0]), (CELLS, halos[1])):
+        arrived(c)
+        copy.start()
+    for c in range(2, CELLS):
+        arrived(c)
+
     then = Forces(lambda c: back_x[c], used_of, *scratch)
-    then.cells(lambda i: i + 1, CELLS)
+    then.cells(lambda i: i + 2, CELLS - 2)
+    for copy in halos:
+        copy.wait()
+    then.cells(lambda i: CELLS - (CELLS - 1) * i, 2)
     then.first_halo()
     inner = bonds([plane(back_x_rows, 8, k) for k in range(3)], used_ox)
     pltpu.make_async_copy(back_v, back_v, v_recv).wait()
@@ -546,14 +561,9 @@
     pltpu.make_async_copy(mode_out.at[0], mode_out.at[0], out_send.at[0]).wait()
     pltpu.make_async_copy(mode_out.at[1], mode_out.at[1], out_send.at[1]).wait()
 
-    @pl.when((b == 0) | (b == GROUP - 1))
-    def _():
-        pltpu.make_async_copy(mode_out.at[0], mode_out.at[0], out_send.at[2]).wait()
-
 
 def local(positions, momenta, molecules):
-    ids = jnp.transpose(molecules, (0, 2, 1)).reshape(CELLS, 3 * MOLS)
-    ids = jnp.pad(ids, ((0, 0), (0, SLOTS - 3 * MOLS)), constant_values=SLOTS)
+    ids = jnp.transpose(molecules, (2, 0, 1))
     first, second = propagators()
     vmem = pl.BlockSpec(memory_space=pltpu.VMEM)
     return pl.pallas_call(
@@ -579,16 +589,16 @@
             pltpu.VMEM((2, GROUP, 8, SLOTS), f32),
             pltpu.VMEM((CELLS + 2, 8, SLOTS), f32),
             pltpu.VMEM((CELLS, 8, SLOTS), f32),
+            pltpu.SemaphoreType.DMA((4,)),
+            pltpu.SemaphoreType.DMA((4,)),
             pltpu.SemaphoreType.DMA((2,)),
             pltpu.SemaphoreType.DMA((2,)),
             pltpu.SemaphoreType.DMA((2,)),
-            pltpu.SemaphoreType.DMA((2,)),
-            pltpu.SemaphoreType.DMA((3,)),
             pltpu.SemaphoreType.DMA((CELLS + 2,)),
             pltpu.SemaphoreType.DMA,
         ],
         compiler_params=pltpu.CompilerParams(collective_id=0, has_side_effects=True),
-    )(positions, momenta, ids, jnp.asarray(first), jnp.asarray(second))
+    )(positions, momenta, ids, thirds(first), thirds(second))
 
 
 def solution(mesh):

time: 55.3 us -> 47 us (0.85)
  Pallas kernels: 50.9 us -> 44.1 us
  local copies, waits for them, and re-layouts: 3.5 us -> 2.06 us
    pallas_call x1, Pallas kernels: 50.9 us -> 44.1 us  [local(): pl.pallas_call(kernel, out_shape=[jax.ShapeDtypeStruct(positions.shape, f...]
    transpose x1 -> x0, local copies, waits for them, and re-layouts: 0.75 us -> none  [local(): ids = jnp.transpose(molecules, (0, 2, 1)).reshape(CELLS, 3 * MOLS)]
    pad x1 -> x0, local copies, waits for them, and re-layouts: 0.61 us -> none  [local(): ids = jnp.pad(ids, ((0, 0), (0, SLOTS - 3 * MOLS)), constant_values=SLOTS)]
where the time goes in v3:
time: 47 us; the launch traced here: 46.8 us
  Pallas kernels  44.1 us (94%)
  local copies, waits for them, and re-layouts  2.06 us (4%)
  between operations  0.65 us (1%)
    pallas_call x1, Pallas kernels, local(): pl.pallas_call(kernel, out_shape=[jax.ShapeDtypeStruct(positions.shape, f...  44.1 us
    unnamed x4, local copies, waits for them, and re-layouts  2.06 us

profile of v3, /device:TPU:2, one launch (start us, length us, event | category | flops | bytes accessed | tf_op | source)
XLA Modules:
  0.0 46.8 jit_solution(3975773761746726525)
XLA Ops:
  0.6 44.1 %shard_map.68 = (f32[2,3,16,128]{3,2,1,0:T(8,128)}, f32[2,3,16,128]{3,2,1,0:T(8,128)}) custom-call(f32[2,3,16,128]{3,2,1,0:T(8,128)} %pos_ref.1, f32[2,3,16,128]{3,2,1,0:T(8,128)} %mom_ref.1, s32[3,16,42]{2,1,0:T(8,128)} %bitcast.1, bf16[3,192,256]{2,1,0:T(8,128)(2,1)} %constant.19.first_ref, bf16[3,256,192]{2,1,0:T(8,128)(2,1)} %constant.30.second_ref), custom_call_target="tpu_custom_call" | custom-call | tf_op jit(solution)/shard_map/pallas_call | solution.py:569
  44.7 0.0 copy-start
  44.7 1.4 %copy.9 = f32[2,3,16,128]{3,2,1,0:T(8,128)} copy(f32[2,3,16,128]{3,2,1,0:T(8,128)} %get-tuple-element.4) | data formatting | bytes 98304
  46.2 0.0 copy-done
  46.2 0.6 %copy.10 = f32[2,3,16,128]{3,2,1,0:T(8,128)} copy(f32[2,3,16,128]{3,2,1,0:T(8,128)S(1)} %copy-done) | data formatting | bytes 98304
Async XLA Ops:
  44.7 1.4 %copy-start = (f32[2,3,16,128]{3,2,1,0:T(8,128)S(1)}, f32[2,3,16,128]{3,2,1,0:T(8,128)}, u32[]{:S(2)}) copy-start(f32[2,3,16,128]{3,2,1,0:T(8,128)} %get-tuple-element.5) | copy-start | bytes 147460

commit v4 on v3

--- a/solution.py
+++ b/solution.py
@@ -16,6 +16,9 @@
 BEADS = 32
 GROUP = 16
 SPACE = 32
+KEEPERS = ((0, 3, 1, 2), (0, 0, 1, 1))
+GREET_MID = (0, 1)
+ROWS = (7, 6)
 FLIP = 16
 
 charge_oxygen = -0.8476
@@ -67,7 +70,7 @@
     for kind in range(2):
         for k in range(3):
             for j in range(BEADS):
-                tile[kind, k, j] = 128 * kind + 8 * (j // 2) + 4 * (j % 2) + k
+                tile[kind, k, j] = 128 * kind + 8 * (j // 2) + 3 * (j % 2) + k
                 plane[kind, k, j] = 96 * kind + 32 * k + j
     first = np.zeros((192, 256))
     second = np.zeros((256, 192))
@@ -122,7 +125,7 @@
     both = jnp.concatenate([high, mid], axis=1)
     out = dot(matrix_ref[0], both) + dot(matrix_ref[1], both)
     small = dot(matrix_ref[0], low) + dot(matrix_ref[2], high)
-    return out[:, :SLOTS] + (out[:, SLOTS:] + small)
+    return out[:, : x.shape[1]] + (out[:, x.shape[1] :] + small)
 
 
 def rolled(x, shift):
@@ -155,7 +158,7 @@
 
 def bead_rows(bead):
     row = lax.broadcasted_iota(jnp.int32, (8, SLOTS), 0)
-    return (row >= 4 * bead) & (row < 4 * bead + 3), row == 4 * bead + 3, row == (4 * bead + 4) % 8
+    return (row >= 3 * bead) & (row < 3 * bead + 3), row == 6, row == 7
 
 
 def left_features(xyz, norm, rows):
@@ -183,7 +186,7 @@
 
 
 def pulled(xyz, sums, bead):
-    return xyz * sums[4 * bead + 3 : 4 * bead + 4, :] - sums
+    return xyz * sums[6:7, :] - sums
 
 
 def folded(out):
@@ -204,7 +207,7 @@
         self.lane = lax.broadcasted_iota(jnp.int32, (8, SLOTS), 1)
 
     def xyz(self, c, bead, cell_shift):
-        shift = jnp.where(self.row == 4 * bead, 0.5 - cell_shift, 0.5)
+        shift = jnp.where(self.row == 3 * bead, 0.5 - cell_shift, 0.5)
         return jnp.where(self.rows[bead][0], self.tile_of(c) - shift, 0.0)
 
     def squares(self, c, bead, alone=False):
@@ -280,7 +283,7 @@
         for bead in range(2):
             y = lax.rsqrt(self.near_ref[bead, :, SLOTS:])
             out.append(self.next_sums(0, bead, split2(y * y * y)))
-        self.next_ref[1] = jnp.where(self.row < 4, out[0], out[1])
+        self.next_ref[1] = jnp.where(self.row < 3, out[0], out[1])
 
     def cells(self, cell_of, count):
         for bead in range(2):
@@ -293,21 +296,85 @@
             self.squares(follows, 0)
             near1, after1 = self.sums(c, 1)
             self.squares(follows, 1)
-            self.own_ref[c] = jnp.where(self.row < 4, near0, near1)
-            self.next_ref[c + 1] = jnp.where(self.row < 4, after0, after1)
+            self.own_ref[c] = jnp.where(self.row < 3, near0, near1)
+            self.next_ref[c + 1] = jnp.where(self.row < 3, after0, after1)
             return carry
 
         lax.fori_loop(0, count, body, 0, unroll=2)
 
 
+def evolve(first_ref, second_ref, mode_in, mode_out, back_x, back_v, in_recv, out_send, out_recv, v_recv, cells, slots, group):
+    b = lax.axis_index("bead")
+    is_oxygen, _ = patterns()
+    for kind in range(2):
+        received = mode_in.at[kind, pl.ds(0, slots), :, pl.ds(0, ROWS[kind])]
+        pltpu.make_async_copy(received, received, in_recv.at[kind]).wait()
+    rows = [mode_in[:, slot].reshape(256, SLOTS) for slot in range(slots)]
+    evolved = by_thirds(first_ref, jnp.concatenate(rows, axis=1))
+    states = []
+    for slot in range(slots):
+        oxygens = mode_in[0, slot, 0, 6:7, :] * is_oxygen
+        inverse = 1.0 - (15.0 / 16.0) * oxygens
+        mine = evolved[:, SLOTS * slot : SLOTS * slot + SLOTS]
+        pull = bonds([mine[32 * k : 32 * k + 32] for k in range(3)], oxygens)
+        kicked = [mine[96 + 32 * k : 128 + 32 * k] + (inner_step * inverse) * pull[k] for k in range(3)]
+        states.append(jnp.concatenate([mine[:96], *kicked], axis=0))
+    out = by_thirds(second_ref, jnp.concatenate(states, axis=1))
+    for slot in range(slots):
+        mode_out[:, slot] = out[:, SLOTS * slot : SLOTS * slot + SLOTS].reshape(2, GROUP, 8, SLOTS)
+
+    def back(kind, slot, dst, recv_sem):
+        def send(i, carry):
+            peer = lax.rem(b // 4 + i, 4) * 4 + i // 4
+            pltpu.make_async_remote_copy(
+                src_ref=mode_out.at[kind, slot, peer, pl.ds(0, 6)],
+                dst_ref=dst.at[pl.ds(0, 6)],
+                send_sem=out_send.at[kind],
+                recv_sem=recv_sem,
+                device_id=(peer, group),
+                device_id_type=MESH,
+            ).start()
+            return carry
+
+        lax.fori_loop(0, GROUP, send, 0)
+
+    for slot in range(slots):
+        at = cells[slot]
+        back(0, slot, back_x.at[at + 1], out_recv.at[at + 1])
+    for slot in range(slots):
+        back(1, slot, back_v.at[cells[slot]], v_recv)
+
+
+def pick(group, two):
+    return jnp.where(group < SPACE // 2, two[0], two[1]) != 0
+
+
+def slots_of(row):
+    return [row[:q].count(row[q]) for q in range(4)]
+
+
+def table(group, of, at):
+    rows = [list(of(row)) for row in KEEPERS]
+    out = 0
+    for i in range(4):
+        value = rows[0][i] if rows[0][i] == rows[1][i] else jnp.where(group < SPACE // 2, rows[0][i], rows[1][i])
+        out = value if i == 0 else jnp.where(at == i, value, out)
+    return out
+
+
 def kernel(
+    pos_hbm,
+    mom_hbm,
+    ids_hbm,
+    first_hbm,
+    second_hbm,
+    out,
     pos_ref,
     mom_ref,
     ids_ref,
     first_ref,
     second_ref,
-    x_out,
-    p_out,
+    load_sem,
     raw,
     hot,
     tiles,
@@ -339,11 +406,31 @@
     right = lax.rem(s + 1, SPACE)
     left = lax.rem(s + SPACE - 1, SPACE)
     x_own, z_own = b // 4, lax.rem(b, 4)
-    late = z_own >= 2
-    z_far = z_own + jnp.where(s < SPACE // 2, 1, 2)
-
-    def far_first(i):
-        return lax.rem(x_own + 2 + lax.rem(i, 4), 4) * 4 + lax.rem(z_far + i // 4, 4)
+    late = (z_own >= 2) | ((z_own == 1) & pick(s, GREET_MID))
+
+    from_cell = jnp.where(z_own == 0, 8, 0)
+
+    def keeper(j):
+        return lax.rem(j, 4) * 4 + table(s, lambda row: row, j // 4)
+
+    def slot_of(j):
+        return table(s, slots_of, j // 4)
+
+    kept = table(far, lambda row: [row.count(z) for z in range(4)], z_own)
+    kept_cells = [
+        x_own + 4 * table(far, lambda row: [([q for q in range(4) if row[q] == z] + [0, 0])[k] for z in range(4)], z_own)
+        for k in range(2)
+    ]
+    senders = table(s, lambda row: [4 * len(set(row))] * 4, 0)
+
+    loads = [
+        pltpu.make_async_copy(src, dst, load_sem.at[i])
+        for i, (src, dst) in enumerate(
+            ((pos_hbm, pos_ref), (mom_hbm, mom_ref), (ids_hbm, ids_ref), (first_hbm, first_ref), (second_hbm, second_ref))
+        )
+    ]
+    for load in loads:
+        load.start()
 
     barrier = pltpu.get_barrier_semaphore()
 
@@ -351,15 +438,23 @@
         pl.semaphore_signal(barrier, inc=1, device_id=(peer, far), device_id_type=MESH)
         return carry
 
-    lax.fori_loop(0, GROUP, hello, 0)
+    mode_in[...] = jnp.zeros_like(mode_in)
+
+    @pl.when(kept > 0)
+    def _():
+        lax.fori_loop(0, GROUP, hello, 0)
+
     for who in (left, right):
         pl.semaphore_signal(barrier, inc=1, device_id=(b, who), device_id_type=MESH)
+
+    for load in loads[:3]:
+        load.wait()
 
     raw[...] = jnp.zeros_like(raw)
     for bead in range(2):
         for k in range(3):
-            raw[pl.ds(4 * bead + k, CELLS, stride=16), :] = pos_ref[bead, k]
-            raw[pl.ds(8 + 4 * bead + k, CELLS, stride=16), :] = mom_ref[bead, k]
+            raw[pl.ds(3 * bead + k, CELLS, stride=16), :] = pos_ref[bead, k]
+            raw[pl.ds(8 + 3 * bead + k, CELLS, stride=16), :] = mom_ref[bead, k]
 
     sub = lax.broadcasted_iota(jnp.int32, (SLOTS, SLOTS), 0)
     lane = lax.broadcasted_iota(jnp.int32, (SLOTS, SLOTS), 1)
@@ -394,23 +489,23 @@
         place = jnp.where((sub_f == key) | (spare_key == key), 1.0, 0.0).astype(bf16)
         hot[c] = place
         rows = moved_exactly(raw[16 * c : 16 * c + 16], place, dot)
-        rows = jnp.where(row16 == 3, used_all[c : c + 1], rows)
+        rows = jnp.where(row16 == 6, used_all[c : c + 1], rows)
         tiles[c + 1] = rows[:8]
         moms[c] = rows[8:]
 
-    def beside(first, last, below, above, at):
+    def beside(ref, rows, at):
         return [
             pltpu.make_async_remote_copy(
-                src_ref=first,
-                dst_ref=above,
+                src_ref=ref.at[1, pl.ds(0, rows)],
+                dst_ref=ref.at[CELLS + 1, pl.ds(0, rows)],
                 send_sem=halo_send.at[at],
                 recv_sem=halo_recv.at[at],
                 device_id=(b, left),
                 device_id_type=MESH,
             ),
             pltpu.make_async_remote_copy(
-                src_ref=last,
-                dst_ref=below,
+                src_ref=ref.at[CELLS, pl.ds(0, rows)],
+                dst_ref=ref.at[0, pl.ds(0, rows)],
                 send_sem=halo_send.at[at + 1],
                 recv_sem=halo_recv.at[at + 1],
                 device_id=(b, right),
@@ -420,26 +515,25 @@
 
     def send_in(kind, ref, first):
         def send(i, carry):
-            peer = far_first(i)
+            j = lax.rem(from_cell + i, CELLS)
             pltpu.make_async_remote_copy(
-                src_ref=ref.at[peer + first],
-                dst_ref=mode_in.at[kind, b],
+                src_ref=ref.at[j + first, pl.ds(0, ROWS[kind])],
+                dst_ref=mode_in.at[kind, slot_of(j), b, pl.ds(0, ROWS[kind])],
                 send_sem=in_send.at[kind],
                 recv_sem=in_recv.at[kind],
-                device_id=(peer, far),
+                device_id=(keeper(j), far),
                 device_id_type=MESH,
             ).start()
             return carry
 
         lax.fori_loop(0, GROUP, send, 0)
 
-    halos = beside(tiles.at[1], tiles.at[CELLS], tiles.at[0], tiles.at[CELLS + 1], 0)
+    halos = beside(tiles, 7, 0)
 
     def greet():
-        pl.semaphore_wait(barrier, GROUP + 2)
+        pl.semaphore_wait(barrier, senders + 2)
         for copy in halos:
             copy.start()
-        send_in(0, tiles, 1)
 
     is_oxygen, _ = patterns()
     used_planes = jnp.concatenate([used_all, used_all], axis=0)
@@ -448,7 +542,7 @@
     mass = 1.0 + 15.0 * used_ox
 
     def used_of(c):
-        return tiles[c, 3:4, :]
+        return tiles[c, 6:7, :]
 
     tiles_rows = tiles.reshape((CELLS + 2) * 8, SLOTS)
     moms_rows = moms.reshape(CELLS * 8, SLOTS)
@@ -460,17 +554,26 @@
 
     def plane(ref, start, k):
         return jnp.concatenate(
-            [ref[pl.ds(start + 4 * bead + k, CELLS, stride=8), :] for bead in range(2)], axis=0
+            [ref[pl.ds(start + 3 * bead + k, CELLS, stride=8), :] for bead in range(2)], axis=0
         )
 
     scratch = (own_ref, next_ref, mask_ref, lj_mask_ref, near_ref, ox_ref, feats_ref, ox_feats_ref)
     now = Forces(lambda c: tiles[c], used_of, *scratch)
     now.cells(lambda i: i + 2, 4)
-    pl.when(late)(greet)
+    @pl.when(late)
+    def _():
+        greet()
+        send_in(0, tiles, 1)
+
     now.cells(lambda i: i + 6, CELLS - 6)
     pl.when(jnp.logical_not(late))(greet)
     for copy in halos:
         copy.wait()
+
+    @pl.when(jnp.logical_not(late))
+    def _():
+        send_in(0, tiles, 1)
+
     now.cells(lambda i: CELLS - (CELLS - 1) * i, 2)
     now.first_halo()
     inner = bonds([plane(tiles_rows, 8, k) for k in range(3)], used_ox)
@@ -480,68 +583,44 @@
         p = plane(moms_rows, 0, k) + (0.5 * outer_step) * outer
         v = (p + (0.5 * inner_step) * inner[k]) * inverse_mass
         for bead in range(2):
-            sent_rows[pl.ds(4 * bead + k, CELLS, stride=8), :] = v[CELLS * bead : CELLS * bead + CELLS]
+            sent_rows[pl.ds(3 * bead + k, CELLS, stride=8), :] = v[CELLS * bead : CELLS * bead + CELLS]
 
     send_in(1, sent_v, 0)
 
-    def all_of(kind, ref, send_sem, recv_sem):
-        return pltpu.make_async_remote_copy(
-            src_ref=ref,
-            dst_ref=mode_in.at[kind],
-            send_sem=send_sem,
-            recv_sem=recv_sem,
-            device_id=(b, far),
-            device_id_type=MESH,
-        )
-
-    all_of(0, tiles.at[pl.ds(1, CELLS)], in_send.at[0], in_recv.at[0]).wait()
-    all_of(1, sent_v, in_send.at[1], in_recv.at[1]).wait()
-
-    mode_rows = mode_in[...].reshape(256, SLOTS)
-    mode_ox = mode_in[0, 0, 3:4, :] * is_oxygen
-    mode_inverse = 1.0 - (15.0 / 16.0) * mode_ox
-    evolved = by_thirds(first_ref, mode_rows)
-    pull = bonds([evolved[32 * k : 32 * k + 32] for k in range(3)], mode_ox)
-    kicked = [evolved[96 + 32 * k : 128 + 32 * k] + (inner_step * mode_inverse) * pull[k] for k in range(3)]
-    state = jnp.concatenate([evolved[:96], *kicked], axis=0)
-    mode_out[...] = by_thirds(second_ref, state).reshape(2, GROUP, 8, SLOTS)
-
-    def back(kind, dst, recv_sem):
-        def send(i, carry):
-            peer = far_first(i)
-            pltpu.make_async_remote_copy(
-                src_ref=mode_out.at[kind, peer],
-                dst_ref=dst,
-                send_sem=out_send.at[kind],
-                recv_sem=recv_sem,
-                device_id=(peer, far),
-                device_id_type=MESH,
-            ).start()
-            return carry
-
-        lax.fori_loop(0, GROUP, send, 0)
-
-    back(0, back_x.at[b + 1], out_recv.at[b + 1])
-    back(1, back_v.at[b], v_recv)
+    evolution = (first_ref, second_ref, mode_in, mode_out, back_x, back_v, in_recv, out_send, out_recv, v_recv)
+
+    for load in loads[3:]:
+        load.wait()
+
+    for count in range(1, 3):
+
+        @pl.when(kept == count)
+        def _():
+            evolve(*evolution, kept_cells, count, far)
 
     def arrived(c):
-        pltpu.make_async_copy(back_x.at[c], back_x.at[c], out_recv.at[c]).wait()
-
-    halos = beside(back_x.at[1], back_x.at[CELLS], back_x.at[0], back_x.at[CELLS + 1], 2)
-    for c, copy in ((1, halos[0]), (CELLS, halos[1])):
+        tile = back_x.at[c, pl.ds(0, 6)]
+        pltpu.make_async_copy(tile, tile, out_recv.at[c]).wait()
+
+    halos = beside(back_x, 6, 2)
+    arrived(1)
+    halos[0].start()
+    for c in range(2, 9):
         arrived(c)
-        copy.start()
-    for c in range(2, CELLS):
+    then = Forces(lambda c: back_x[c], used_of, *scratch)
+    then.cells(lambda i: i + 2, 6)
+    for c in range(CELLS, 8, -1):
         arrived(c)
-
-    then = Forces(lambda c: back_x[c], used_of, *scratch)
-    then.cells(lambda i: i + 2, CELLS - 2)
+        if c == CELLS:
+            halos[1].start()
+    then.cells(lambda i: i + 8, 8)
     for copy in halos:
         copy.wait()
     then.cells(lambda i: CELLS - (CELLS - 1) * i, 2)
     then.first_halo()
     inner = bonds([plane(back_x_rows, 8, k) for k in range(3)], used_ox)
-    pltpu.make_async_copy(back_v, back_v, v_recv).wait()
+    received = back_v.at[:, pl.ds(0, 6)]
+    pltpu.make_async_copy(received, received, v_recv).wait()
     for k in range(3):
         outer = plane(own_rows, 8, k) + plane(next_rows, 8, k)
         p = mass * plane(back_v_rows, 0, k) + (0.5 * inner_step) * inner[k]
@@ -549,29 +628,44 @@
         x = plane(back_x_rows, 8, k)
         for bead in range(2):
             half = slice(CELLS * bead, CELLS * bead + CELLS)
-            raw[pl.ds(4 * bead + k, CELLS, stride=16), :] = x[half]
-            raw[pl.ds(8 + 4 * bead + k, CELLS, stride=16), :] = p[half]
+            raw[pl.ds(3 * bead + k, CELLS, stride=16), :] = x[half]
+            raw[pl.ds(8 + 3 * bead + k, CELLS, stride=16), :] = p[half]
     for c in range(CELLS):
         raw[16 * c : 16 * c + 16] = moved_exactly(raw[16 * c : 16 * c + 16], hot[c], dot_nt)
     for bead in range(2):
         for k in range(3):
-            x_out[bead, k] = raw[pl.ds(4 * bead + k, CELLS, stride=16), :]
-            p_out[bead, k] = raw[pl.ds(8 + 4 * bead + k, CELLS, stride=16), :]
-
-    pltpu.make_async_copy(mode_out.at[0], mode_out.at[0], out_send.at[0]).wait()
-    pltpu.make_async_copy(mode_out.at[1], mode_out.at[1], out_send.at[1]).wait()
+            out[0, bead, k] = raw[pl.ds(3 * bead + k, CELLS, stride=16), :]
+            out[1, bead, k] = raw[pl.ds(8 + 3 * bead + k, CELLS, stride=16), :]
+
+    for kind in range(2):
+        sent = sent_v.at[:, pl.ds(0, ROWS[kind])]
+        pltpu.make_async_copy(sent, sent, in_send.at[kind]).wait()
+
+    def all_back(slots):
+        for kind in range(2):
+            sent = mode_out.at[kind, pl.ds(0, slots), :, pl.ds(0, 6)]
+            pltpu.make_async_copy(sent, sent, out_send.at[kind]).wait()
+
+    for count in range(1, 3):
+        pl.when(kept == count)(functools.partial(all_back, count))
 
 
 def local(positions, momenta, molecules):
     ids = jnp.transpose(molecules, (2, 0, 1))
     first, second = propagators()
     vmem = pl.BlockSpec(memory_space=pltpu.VMEM)
-    return pl.pallas_call(
+    both = pl.pallas_call(
         kernel,
-        out_shape=[jax.ShapeDtypeStruct(positions.shape, f32)] * 2,
-        in_specs=[vmem] * 5,
-        out_specs=[vmem] * 2,
+        out_shape=jax.ShapeDtypeStruct((2, *positions.shape), f32),
+        in_specs=[pl.BlockSpec(memory_space=pl.ANY)] * 5,
+        out_specs=vmem,
         scratch_shapes=[
+            pltpu.VMEM(positions.shape, f32),
+            pltpu.VMEM(momenta.shape, f32),
+            pltpu.VMEM(ids.shape, jnp.int32),
+            pltpu.VMEM((3, 192, 256), bf16),
+            pltpu.VMEM((3, 256, 192), bf16),
+            pltpu.SemaphoreType.DMA((5,)),
             pltpu.VMEM((CELLS * 16, SLOTS), f32),
             pltpu.VMEM((CELLS, SLOTS, SLOTS), bf16),
             pltpu.VMEM((CELLS + 2, 8, SLOTS), f32),
@@ -585,8 +679,8 @@
             pltpu.VMEM((2, 16, 2 * SLOTS), bf16),
             pltpu.VMEM((2, 16, SLOTS), bf16),
             pltpu.VMEM((CELLS, 8, SLOTS), f32),
-            pltpu.VMEM((2, GROUP, 8, SLOTS), f32),
-            pltpu.VMEM((2, GROUP, 8, SLOTS), f32),
+            pltpu.VMEM((2, 2, GROUP, 8, SLOTS), f32),
+            pltpu.VMEM((2, 2, GROUP, 8, SLOTS), f32),
             pltpu.VMEM((CELLS + 2, 8, SLOTS), f32),
             pltpu.VMEM((CELLS, 8, SLOTS), f32),
             pltpu.SemaphoreType.DMA((4,)),
@@ -599,6 +693,7 @@
         ],
         compiler_params=pltpu.CompilerParams(collective_id=0, has_side_effects=True),
     )(positions, momenta, ids, thirds(first), thirds(second))
+    return both[0], both[1]
 
 
 def solution(mesh):

time: 47 us -> 43.7 us (0.930)
  Pallas kernels: 44.1 us -> 41.4 us
  local copies, waits for them, and re-layouts: 2.06 us -> 1.46 us
    pallas_call x1, Pallas kernels: 44.1 us -> 41.4 us  [local(): pl.pallas_call(kernel, out_shape=jax.ShapeDtypeStruct((2, *positions.shap...]
    unnamed x4 -> x0, local copies, waits for them, and re-layouts: 2.06 us -> none
    squeeze x0 -> x1, local copies, waits for them, and re-layouts: none -> 1.46 us  [local(): return (both[0], both[1])]
where the time goes in v4:
time: 43.7 us; the launch traced here: 43.5 us
  Pallas kernels  41.4 us (95%)
  local copies, waits for them, and re-layouts  1.46 us (3%)
  between operations  0.64 us (1%)
    pallas_call x1, Pallas kernels, local(): pl.pallas_call(kernel, out_shape=jax.ShapeDtypeStruct((2, *positions.shap...  41.4 us
    squeeze x1, local copies, waits for them, and re-layouts, local(): return (both[0], both[1])  1.46 us

profile of v4, /device:TPU:2, one launch (start us, length us, event | category | flops | bytes accessed | tf_op | source)
XLA Modules:
  0.0 43.5 jit_solution(6993391600176794373)
XLA Ops:
  0.6 41.4 %shard_map.68 = f32[2,2,3,16,128]{4,3,2,1,0:T(8,128)} custom-call(f32[2,3,16,128]{3,2,1,0:T(8,128)} %pos_hbm.1, f32[2,3,16,128]{3,2,1,0:T(8,128)} %mom_hbm.1, s32[3,16,42]{2,1,0:T(8,128)} %bitcast.5, bf16[3,192,256]{2,1,0:T(8,128)(2,1)} %constant.19.first_hbm, bf16[3,256,192]{2,1,0:T(8,128)(2,1)} %constant.30.second_hbm), custom_call_target="tpu_custom_call" | custom-call | tf_op jit(solution)/shard_map/pallas_call | solution.py:657
  42.0 1.5 %slice_bitcast_fusion = (f32[2,3,16,128]{3,2,1,0:T(8,128)}, f32[2,3,16,128]{3,2,1,0:T(8,128)}) fusion(f32[2,2,3,16,128]{4,3,2,1,0:T(8,128)} %shard_map.68), kind=kLoop, calls=%fused_computation | loop fusion | bytes 196608 | tf_op jit(solution)/shard_map/squeeze | solution.py:696

commit v5 on v4

--- a/solution.py
+++ b/solution.py
@@ -16,7 +16,7 @@
 BEADS = 32
 GROUP = 16
 SPACE = 32
-KEEPERS = ((0, 3, 1, 2), (0, 0, 1, 1))
+KEEPERS = ((0, 3, 1, 2), (0, 1, 1, 3))
 GREET_MID = (0, 1)
 ROWS = (7, 6)
 FLIP = 16
@@ -513,9 +513,9 @@
             ),
         ]
 
-    def send_in(kind, ref, first):
+    def send_in(kind, ref, first, cell_of, count):
         def send(i, carry):
-            j = lax.rem(from_cell + i, CELLS)
+            j = cell_of(i)
             pltpu.make_async_remote_copy(
                 src_ref=ref.at[j + first, pl.ds(0, ROWS[kind])],
                 dst_ref=mode_in.at[kind, slot_of(j), b, pl.ds(0, ROWS[kind])],
@@ -526,7 +526,10 @@
             ).start()
             return carry
 
-        lax.fori_loop(0, GROUP, send, 0)
+        lax.fori_loop(0, count, send, 0)
+
+    def send_x():
+        send_in(0, tiles, 1, lambda i: lax.rem(from_cell + i, CELLS), CELLS)
 
     halos = beside(tiles, 7, 0)
 
@@ -557,35 +560,45 @@
             [ref[pl.ds(start + 3 * bead + k, CELLS, stride=8), :] for bead in range(2)], axis=0
         )
 
+    own_ref[...] = jnp.zeros_like(own_ref)
+    next_ref[...] = jnp.zeros_like(next_ref)
     scratch = (own_ref, next_ref, mask_ref, lj_mask_ref, near_ref, ox_ref, feats_ref, ox_feats_ref)
     now = Forces(lambda c: tiles[c], used_of, *scratch)
     now.cells(lambda i: i + 2, 4)
     @pl.when(late)
     def _():
         greet()
-        send_in(0, tiles, 1)
+        send_x()
 
     now.cells(lambda i: i + 6, CELLS - 6)
     pl.when(jnp.logical_not(late))(greet)
+
+    @pl.when(jnp.logical_not(late))
+    def _():
+        send_x()
+
+    inner = bonds([plane(tiles_rows, 8, k) for k in range(3)], used_ox)
+
+    def kicked():
+        out = []
+        for k in range(3):
+            p = plane(moms_rows, 0, k) + (0.5 * outer_step) * (plane(own_rows, 8, k) + plane(next_rows, 8, k))
+            out.append((p + (0.5 * inner_step) * inner[k]) * inverse_mass)
+        return out
+
+    for k, v in enumerate(kicked()):
+        for bead in range(2):
+            sent_rows[pl.ds(3 * bead + k, CELLS, stride=8), :] = v[CELLS * bead : CELLS * bead + CELLS]
+    send_in(1, sent_v, 0, lambda i: 2 + lax.rem(jnp.maximum(from_cell - 2, 0) + i, CELLS - 3), CELLS - 3)
     for copy in halos:
         copy.wait()
-
-    @pl.when(jnp.logical_not(late))
-    def _():
-        send_in(0, tiles, 1)
-
     now.cells(lambda i: CELLS - (CELLS - 1) * i, 2)
     now.first_halo()
-    inner = bonds([plane(tiles_rows, 8, k) for k in range(3)], used_ox)
-    sent_v[...] = jnp.zeros_like(sent_v)
-    for k in range(3):
-        outer = plane(own_rows, 8, k) + plane(next_rows, 8, k)
-        p = plane(moms_rows, 0, k) + (0.5 * outer_step) * outer
-        v = (p + (0.5 * inner_step) * inner[k]) * inverse_mass
+    for k, v in enumerate(kicked()):
         for bead in range(2):
-            sent_rows[pl.ds(3 * bead + k, CELLS, stride=8), :] = v[CELLS * bead : CELLS * bead + CELLS]
-
-    send_in(1, sent_v, 0)
+            for c in (0, 1, CELLS - 1):
+                sent_v[c, 3 * bead + k : 3 * bead + k + 1, :] = v[CELLS * bead + c : CELLS * bead + c + 1]
+    send_in(1, sent_v, 0, lambda i: jnp.where(i == 2, CELLS - 1, i), 3)
 
     evolution = (first_ref, second_ref, mode_in, mode_out, back_x, back_v, in_recv, out_send, out_recv, v_recv)
 

time: 43.7 us -> 43 us (0.984)
  Pallas kernels: 41.4 us -> 40.7 us
    pallas_call x1, Pallas kernels: 41.4 us -> 40.7 us  [local(): pl.pallas_call(kernel, out_shape=jax.ShapeDtypeStruct((2, *positions.shap...]
where the time goes in v5:
time: 43 us; the launch traced here: 42.8 us
  Pallas kernels  40.7 us (95%)
  local copies, waits for them, and re-layouts  1.46 us (3%)
  between operations  0.64 us (1%)
    pallas_call x1, Pallas kernels, local(): pl.pallas_call(kernel, out_shape=jax.ShapeDtypeStruct((2, *positions.shap...  40.7 us
    squeeze x1, local copies, waits for them, and re-layouts, local(): return (both[0], both[1])  1.46 us

profile of v5, /device:TPU:2, one launch (start us, length us, event | category | flops | bytes accessed | tf_op | source)
XLA Modules:
  0.0 42.8 jit_solution(7488599108657488024)
XLA Ops:
  0.6 40.7 %shard_map.68 = f32[2,2,3,16,128]{4,3,2,1,0:T(8,128)} custom-call(f32[2,3,16,128]{3,2,1,0:T(8,128)} %pos_hbm.1, f32[2,3,16,128]{3,2,1,0:T(8,128)} %mom_hbm.1, s32[3,16,42]{2,1,0:T(8,128)} %bitcast.5, bf16[3,192,256]{2,1,0:T(8,128)(2,1)} %constant.19.first_hbm, bf16[3,256,192]{2,1,0:T(8,128)(2,1)} %constant.30.second_hbm), custom_call_target="tpu_custom_call" | custom-call | tf_op jit(solution)/shard_map/pallas_call | solution.py:670
  41.4 1.5 %slice_bitcast_fusion = (f32[2,3,16,128]{3,2,1,0:T(8,128)}, f32[2,3,16,128]{3,2,1,0:T(8,128)}) fusion(f32[2,2,3,16,128]{4,3,2,1,0:T(8,128)} %shard_map.68), kind=kLoop, calls=%fused_computation | loop fusion | bytes 196608 | tf_op jit(solution)/shard_map/squeeze | solution.py:709

commit v6 on v5

--- a/solution.py
+++ b/solution.py
@@ -319,10 +319,6 @@
         pull = bonds([mine[32 * k : 32 * k + 32] for k in range(3)], oxygens)
         kicked = [mine[96 + 32 * k : 128 + 32 * k] + (inner_step * inverse) * pull[k] for k in range(3)]
         states.append(jnp.concatenate([mine[:96], *kicked], axis=0))
-    out = by_thirds(second_ref, jnp.concatenate(states, axis=1))
-    for slot in range(slots):
-        mode_out[:, slot] = out[:, SLOTS * slot : SLOTS * slot + SLOTS].reshape(2, GROUP, 8, SLOTS)
-
     def back(kind, slot, dst, recv_sem):
         def send(i, carry):
             peer = lax.rem(b // 4 + i, 4) * 4 + i // 4
@@ -338,11 +334,17 @@
 
         lax.fori_loop(0, GROUP, send, 0)
 
-    for slot in range(slots):
-        at = cells[slot]
-        back(0, slot, back_x.at[at + 1], out_recv.at[at + 1])
-    for slot in range(slots):
-        back(1, slot, back_v.at[cells[slot]], v_recv)
+    state = jnp.concatenate(states, axis=1)
+    for kind in range(2):
+        out = by_thirds(second_ref.at[:, pl.ds(128 * kind, 128)], state)
+        for slot in range(slots):
+            mode_out[kind, slot] = out[:, SLOTS * slot : SLOTS * slot + SLOTS].reshape(GROUP, 8, SLOTS)
+        for slot in range(slots):
+            at = cells[slot]
+            if kind == 0:
+                back(0, slot, back_x.at[at + 1], out_recv.at[at + 1])
+            else:
+                back(1, slot, back_v.at[at], v_recv)
 
 
 def pick(group, two):

time: 43 us -> 43 us (level)
  no operation moved by 1% of the time
where the time goes in v6:
time: 43 us; the launch traced here: 42.8 us
  Pallas kernels  40.7 us (95%)
  local copies, waits for them, and re-layouts  1.46 us (3%)
  between operations  0.64 us (1%)
    pallas_call x1, Pallas kernels, local(): pl.pallas_call(kernel, out_shape=jax.ShapeDtypeStruct((2, *positions.shap...  40.7 us
    squeeze x1, local copies, waits for them, and re-layouts, local(): return (both[0], both[1])  1.46 us

profile of v6, /device:TPU:2, one launch (start us, length us, event | category | flops | bytes accessed | tf_op | source)
XLA Modules:
  0.0 42.8 jit_solution(2459877611339524439)
XLA Ops:
  0.6 40.7 %shard_map.68 = f32[2,2,3,16,128]{4,3,2,1,0:T(8,128)} custom-call(f32[2,3,16,128]{3,2,1,0:T(8,128)} %pos_hbm.1, f32[2,3,16,128]{3,2,1,0:T(8,128)} %mom_hbm.1, s32[3,16,42]{2,1,0:T(8,128)} %bitcast.5, bf16[3,192,256]{2,1,0:T(8,128)(2,1)} %constant.19.first_hbm, bf16[3,256,192]{2,1,0:T(8,128)(2,1)} %constant.30.second_hbm), custom_call_target="tpu_custom_call" | custom-call | tf_op jit(solution)/shard_map/pallas_call | solution.py:672
  41.3 1.5 %slice_bitcast_fusion = (f32[2,3,16,128]{3,2,1,0:T(8,128)}, f32[2,3,16,128]{3,2,1,0:T(8,128)}) fusion(f32[2,2,3,16,128]{4,3,2,1,0:T(8,128)} %shard_map.68), kind=kLoop, calls=%fused_computation | loop fusion | bytes 196608 | tf_op jit(solution)/shard_map/squeeze | solution.py:711
